TPU v7x, 32 devices: a whole 2x2x4 slice. The times are simulated.
32 devices in a mesh: loop: 16 (over z, y, core), narrow: 2 (over x).
Axes of the slice: x: 2, y: 2, z: 4, core: 2. Of those that a mesh axis runs over, the one named last changes fastest.
Arguments:
- queries: bfloat16 [8192, 4096], P(('loop', 'narrow')), may hold values from -2 to 2
- passages: bfloat16 [64, 4096], P('loop'), may hold values from -10 to 10
- pos_ids: int32 [8192], P(('loop', 'narrow')), may hold values from 0 to 63
- neg_ids: int32 [8192, 32], P(('loop', 'narrow')), may hold values from 0 to 63
- neg_mask: int32 [8192, 32], P(('loop', 'narrow')), may hold values 0 or 1
- neg_counts: int32 [8192], P(('loop', 'narrow')), may hold values from 0 to 32
- d_loss: float32 [8192], P(('loop', 'narrow')), may hold values from -6 to 6
Outputs:
- query_loss: float32 [8192], P(('loop', 'narrow'))
- grad_queries: bfloat16 [8192, 4096], P(('loop', 'narrow'))
- grad_passages: bfloat16 [64, 4096], P('loop')
Inputs may be any that keep to these rules, and one draw needn't show every extreme that they name: `neg_counts`: slots at or beyond a query's count are padding.
All inputs are finite; a program needn't handle non-finite values. No bound on the sum of `neg_mask` on one device may be relied on, other than what follows from the above.
Results may differ from a plain program's by a relative error of at most 0.0058.
Values may be sent and summed in bfloat16 or wider, within the bound.
No kernel may reach another device: no remote copies, remote signals or barrier semaphores. Data moves between devices by JAX's collectives and lax.ppermute only.
A program may use at most 64 MiB of HBM per device.

v0:
```python
import jax
import jax.numpy as jnp
from jax import lax
from jax.sharding import PartitionSpec as P

NEG = 32


logit_scale = 50.0
norm_eps = 1e-06


def normalize(rows):
    wide = rows.astype(jnp.float32)
    scales = lax.rsqrt(jnp.sum(wide * wide, axis=-1) + norm_eps)
    return (scales, (wide * scales[:, None]).astype(jnp.bfloat16))


def weight_table(valid, neg_ids, pool_size):
    columns = jnp.arange(pool_size, dtype=jnp.int32)
    weights = jnp.ones((neg_ids.shape[0], pool_size), jnp.float32)
    for first in range(0, NEG, 8):
        named = neg_ids[:, first : first + 8]
        usable = valid[:, first : first + 8]
        hits = (named[:, :, None] == columns[None, None, :]) & usable[:, :, None]
        weights = weights + jnp.sum(hits.astype(jnp.float32), axis=1)
    return weights


def tangent_back(rows, scales, direction):
    unit = rows.astype(jnp.float32) * scales[:, None]
    inner = jnp.sum(unit * direction, axis=-1, keepdims=True)
    return (scales[:, None] * (direction - unit * inner)).astype(jnp.bfloat16)


def local(queries, passages, pos_ids, neg_ids, neg_mask, neg_counts, d_loss):
    qscale, qnorm = normalize(queries)
    pscale, pnorm = normalize(passages)
    pool = lax.all_gather(pnorm, "loop", axis=0, tiled=True)
    pool_size = pool.shape[0]
    columns = jnp.arange(pool_size, dtype=jnp.int32)
    slots = jnp.arange(NEG, dtype=jnp.int32)
    scores = logit_scale * lax.dot_general(
        qnorm, pool, (((1,), (1,)), ((), ())), preferred_element_type=jnp.float32
    )
    valid = (neg_mask == 1) & (slots[None, :] < neg_counts[:, None])
    weights = weight_table(valid, neg_ids, pool_size)
    terms = weights * jnp.exp(scores)
    denom = jnp.sum(terms, axis=1)
    chosen = columns[None, :] == pos_ids[:, None]
    picked = jnp.sum(jnp.where(chosen, scores, 0.0), axis=1)
    query_loss = jnp.log(denom) - picked
    coef = (
        logit_scale * d_loss[:, None] * (terms / denom[:, None] - chosen.astype(jnp.float32))
    ).astype(jnp.bfloat16)
    qdir = jnp.dot(coef, pool, preferred_element_type=jnp.float32)
    grad_queries = tangent_back(queries, qscale, qdir)
    partial_dir = lax.psum_scatter(
        lax.dot_general(coef, qnorm, (((0,), (0,)), ((), ())), preferred_element_type=jnp.float32),
        "loop",
        scatter_dimension=0,
        tiled=True,
    )
    pdir = lax.psum(partial_dir, "narrow")
    grad_passages = tangent_back(passages, pscale, pdir)
    return (query_loss, grad_queries, grad_passages)


def solution(mesh):
    return jax.shard_map(
        local,
        mesh=mesh,
        in_specs=(
            P(("loop", "narrow"), None),
            P("loop", None),
            P(("loop", "narrow")),
            P(("loop", "narrow"), None),
            P(("loop", "narrow"), None),
            P(("loop", "narrow")),
            P(("loop", "narrow")),
        ),
        out_specs=(P(("loop", "narrow")), P(("loop", "narrow"), None), P("loop", None)),
        check_vma=False,
    )
```

profile of v0, /device:TPU:0, one launch (start us, length us, event | category | flops | bytes accessed | tf_op | source)
XLA Modules:
  0.0 164.1 jit_solution(8291174964269630213)
XLA Ops:
  7.2 0.0 copy-start
  7.2 0.0 copy-start.2
  7.2 0.0 all-reduce.6.cloned.1.call-start
  7.2 1.0 fusion.22
  8.3 2.1 %fusion.7 = f32[256]{0:T(256)S(1)} fusion(bf16[256,4096]{1,0:T(8,128)(2,1)} %param.7), kind=kLoop, calls=%fused_computation.9 | loop fusion | flops 3145472 | bytes 2098176 | tf_op jit(solution)/shard_map/reduce_sum | solution.py:15
  10.4 0.8 fusion.24
  11.2 0.8 fusion.23
  12.0 0.8 fusion.27
  12.8 24.6 %all-gather = bf16[16,4,4096]{2,1,0:T(4,128)(2,1)S(1)} all-gather(bf16[1,4,4096]{2,1,0:T(4,128)(2,1)S(1)} %fusion.23), channel_id=1, replica_groups=mesh['loop'=16,'narrow'=2] {'loop'}, dimensions={0}, use_global_device_ids=true | all-gather | bytes 557056 | tf_op jit(solution)/shard_map/all_gather | solution.py:39
  37.4 0.1 reshape.30
  37.5 0.7 add_rsqrt_fusion
  38.2 0.2 convert_reduce_fusion.2
  38.4 0.2 convert_reduce_fusion
  38.6 0.0 copy-done
  38.6 0.0 copy-done.2
  38.6 0.9 fusion.26
  39.4 1.7 %fusion.8 = f32[64,4096]{1,0:T(8,128)} fusion(bf16[256,4096]{1,0:T(8,128)(2,1)S(1)} %copy-done, f32[256]{0:T(256)S(1)} %get-tuple-element.20, f32[256,64]{0,1:T(8,128)S(1)} %get-tuple-element.4, f32[256]{0:T(256)S(1)} %get-tuple-element.3, f32[256]{0:T(256)S(1)} %get-tuple-element.21, s32[256]{0:T(256)S(1)} %copy-done.2), kind=kOutput, calls=%fused_computation.11 | convolution fusion | flops 137461760 | bytes 3215360 | tf_op jit(solution)/shard_map/dot_general | solution.py:59
  41.1 0.0 all-reduce.6.cloned.1.call-update
  41.1 0.0 all-reduce.4.cloned.1.call-start
  41.2 0.9 fusion.3
  42.1 0.0 copy-start.3
  42.1 0.0 copy-start.1
  42.1 2.5 %fusion.6 = bf16[256,4096]{1,0:T(8,128)(2,1)} fusion(f32[256,4096]{1,0:T(8,128)S(1)} %get-tuple-element.15, bf16[256,4096]{1,0:T(8,128)(2,1)S(1)} %copy-done, f32[256]{0:T(256)S(1)} %get-tuple-element.14, f32[256]{0:T(256)S(1)} %get-tuple-element.20), kind=kLoop, calls=%fused_computation.8 | loop fusion | flops 6291456 | bytes 8390656 | tf_op jit(solution)/shard_map/convert_element_type | solution.py:33
  44.6 0.0 copy-done.3
  44.6 0.6 dynamic-slice
  45.8 86.6 %all-reduce.6.cloned.1.call-done = f32[64,4096]{1,0:T(8,128)} async-done(((f32[64,4096]{1,0:T(8,128)}), f32[64,4096]{1,0:T(8,128)}) %all-reduce.6.cloned.1.call-update) | async-done | bytes 1048592
  132.4 1.5 constant_dynamic-slice_fusion
  133.9 0.0 all-reduce.4.cloned.1.call-update
  133.9 0.6 log_subtract_fusion
  134.5 20.2 %all-reduce.4.cloned.1.call-done = f32[4,4096]{1,0:T(4,128)} async-done(((f32[4,4096]{1,0:T(4,128)}), f32[4,4096]{1,0:T(4,128)}) %all-reduce.4.cloned.1.call-update) | async-done | bytes 65552 | tf_op jit(solution)/shard_map/psum | solution.py:64
  154.7 0.0 copy-done.1
  154.7 1.1 fusion.18
  155.7 1.5 fusion.21
  (2 shorter events, 0.0 us)
Async XLA Ops:
  7.2 31.4 %copy-start = (bf16[256,4096]{1,0:T(8,128)(2,1)S(1)}, bf16[256,4096]{1,0:T(8,128)(2,1)}, u32[]{:S(2)}) copy-start(bf16[256,4096]{1,0:T(8,128)(2,1)} %param.7) | copy-start | bytes 6291460
  7.2 31.4 %copy-start.2 = (s32[256]{0:T(256)S(1)}, s32[256]{0:T(256)}, u32[]{:S(2)}) copy-start(s32[256]{0:T(256)} %param.9) | copy-start | bytes 3076
  7.2 125.2 %all-reduce.6.cloned.1.call-start = ((), (), s32[]{:S(2)}) async-start(), calls=%async_computation.1 | async-start | bytes 2097152
  41.1 113.5 %all-reduce.4.cloned.1.call-start = ((), (), s32[]{:S(2)}) async-start(), calls=%async_computation | async-start | bytes 131072 | tf_op jit(solution)/shard_map/psum | solution.py:64
  42.1 2.5 %copy-start.3 = (u32[32]{0:T(128)S(1)}, u32[32]{0:T(128)}, u32[]{:S(2)}) copy-start(u32[32]{0:T(128)} %constant.15) | copy-start | bytes 388
  42.1 112.6 %copy-start.1 = (bf16[4,4096]{1,0:T(4,128)(2,1)S(1)}, bf16[4,4096]{1,0:T(4,128)(2,1)}, u32[]{:S(2)}) copy-start(bf16[4,4096]{1,0:T(4,128)(2,1)} %param.8) | copy-start | bytes 98308
Sparse Core Ops, SparseCore 0:
  41.3 91.0 all-reduce.5
  134.6 20.0 all-reduce.3
where the time goes:
time: 165 us; the launch traced here: 164 us
  waiting for transfers between devices  107 us (65%)
  blocking collectives  24.6 us (15%)
  between operations  14.8 us (9%)
  other arithmetic  11.5 us (7%)
  matrix products  3.43 us (2%)
  local copies, waits for them, and re-layouts  3.01 us (2%)
    unnamed x3, waiting for transfers between devices  86.6 us
    all_gather x1, blocking collectives, local(): pool = lax.all_gather(pnorm, 'loop', axis=0, tiled=True)  24.6 us
    psum x1, waiting for transfers between devices, local(): pdir = lax.psum(partial_dir, 'narrow')  20.2 us
    convert_element_type x2, other arithmetic, tangent_back(): return (scales[:, None] * (direction - unit * inner)).astype(jnp.bfloat16)  4.01 us
  transfers between devices with their start and end apart: 2, of which 2 were waited for; matrix products, arithmetic and copies ran while one was open for 3% of the time, Pallas kernels for 0%

commit v1 on v0

v1 whole, which is shorter than its diff:
```python
import functools

import jax
import jax.numpy as jnp
from jax import lax
from jax.experimental import pallas as pl
from jax.experimental.pallas import tpu as pltpu
from jax.sharding import PartitionSpec as P


logit_scale = 50.0
norm_eps = 1e-06


LIMIT = pltpu.CompilerParams(vmem_limit_bytes=16 * 1024 * 1024)
WIDE_LIMIT = pltpu.CompilerParams(vmem_limit_bytes=56 * 1024 * 1024)
VMEM = pl.BlockSpec(memory_space=pltpu.VMEM)
SMEM = pl.BlockSpec(memory_space=pltpu.SMEM)
HBM = pl.BlockSpec(memory_space=pltpu.HBM)
F32 = jnp.float32
BF16 = jnp.bfloat16
ROWS = (((1,), (1,)), ((), ()))


def stage_masks(size):
    bits = [1 << b for b in range(size.bit_length() - 1)][::-1]
    first = [0, bits[1] | 1, bits[0] | 1, bits[0] | bits[1] | 1]
    return [first] + [[0, b | 1] for b in bits[2:]]


def swap(x, axis, size, mask):
    return lax.ppermute(x, axis, [(i, i ^ mask) for i in range(size)])


def wide(x):
    return x.astype(F32)


def call(kernel, outs, args, in_specs=None, limit=LIMIT, flops=200000, moved=1000000, **options):
    options.setdefault("out_specs", (VMEM,) * len(outs))
    return pl.pallas_call(
        kernel,
        out_shape=tuple(jax.ShapeDtypeStruct(*out) for out in outs),
        in_specs=in_specs or [VMEM] * len(args),
        cost_estimate=pl.CostEstimate(flops=flops, bytes_accessed=moved, transcendentals=0),
        compiler_params=limit,
        **options,
    )(*args)


def passage_ids(stages, block, shape, me):
    row = lax.broadcasted_iota(jnp.int32, shape, 0)
    place = row // block
    digits, owner = place, jnp.full(shape, me, jnp.int32)
    for masks in stages:
        digit = digits % len(masks)
        digits = digits // len(masks)
        chosen = jnp.zeros(shape, jnp.int32)
        for k, m in enumerate(masks[1:]):
            chosen = jnp.where(digit == k + 1, m, chosen)
        owner = owner ^ chosen
    return owner * block + (row - place * block)


def weight_kernel(stages, block, me_ref, *refs):
    sources, (w_ref, pack_ref), scratch, sems = refs[:5], refs[6:8], refs[8:13], refs[13]
    copies = [pltpu.make_async_copy(src, dst, sems.at[k]) for k, (src, dst) in enumerate(zip(sources, scratch))]
    for copy in copies:
        copy.start()
    half = w_ref.shape[0]
    mine = passage_ids(stages[:-1], block, w_ref.shape, me_ref[0])
    others = passage_ids(stages[:-1], block, w_ref.shape, me_ref[0] ^ stages[-1][1])
    for copy in copies:
        copy.wait()
    ids_ref, mask_ref, count_ref, pos_ref, dl_ref = scratch
    slot = lax.broadcasted_iota(jnp.int32, ids_ref.shape, 0)
    named = jnp.where((mask_ref[...] == 1) & (slot < count_ref[...]), ids_ref[...], -1)
    w_mine = jnp.ones(w_ref.shape, F32)
    w_others = jnp.ones(w_ref.shape, F32)
    for k in range(ids_ref.shape[0]):
        w_mine = w_mine + jnp.where(named[k : k + 1] == mine, 1.0, 0.0)
        w_others = w_others + jnp.where(named[k : k + 1] == others, 1.0, 0.0)
    w_ref[...] = w_mine
    pack_ref[:half] = w_others
    pack_ref[half : half + 1] = dl_ref[...]
    pack_ref[half + 1 : half + 2] = pos_ref[...].astype(F32)
    pack_ref[half + 2 :] = jnp.zeros((6, w_ref.shape[1]), F32)


def raw_and_scale(refs, queries):
    rows = jnp.concatenate([r[...] for r in refs], axis=0)
    f = wide(rows)
    scale = lax.rsqrt(jnp.sum(f * f, axis=1, keepdims=True) + norm_eps)
    raw = [lax.dot_general(rows, q, ROWS, preferred_element_type=F32) for q in queries]
    return rows, jnp.concatenate(raw, axis=1), scale


def early_kernel(n, *refs):
    q_ref, other_ref, raw_ref, scale_ref, qs_ref = refs[n:]
    queries = [q_ref[...], other_ref[...]]
    _, raw, scale = raw_and_scale(refs[:n], queries)
    raw_ref[...] = raw
    scale_ref[...] = jnp.broadcast_to(scale, scale_ref.shape)
    for k, q in enumerate(queries):
        f = wide(q)
        own = lax.rsqrt(jnp.sum(f * f, axis=1, keepdims=True) + norm_eps)
        qs_ref[:, k * q.shape[0] : (k + 1) * q.shape[0]] = jnp.broadcast_to(own, (own.shape[0], 128)).T[:1]


def late_kernel(n, stages, block, me_ref, *refs):
    early, late = refs[: n // 2], refs[n // 2 : n]
    q_ref, other_ref, raw_ref, scale_ref, qs_ref, w_ref, pack_ref, pos_ref = refs[n : n + 8]
    pool_ref, all_ref, scales_ref, terms_ref, chosen_ref, sums_ref = refs[n + 8 :]
    half = w_ref.shape[0]
    rows, raw, scale = raw_and_scale(late, [q_ref[...], other_ref[...]])
    raw = jnp.concatenate([raw_ref[...], raw], axis=0)
    scale = jnp.concatenate([scale_ref[...], jnp.broadcast_to(scale, (scale.shape[0], 128))], axis=0)
    scores = logit_scale * (raw * scale[:, :1] * qs_ref[...])
    terms = jnp.concatenate([w_ref[...], pack_ref[:half]], axis=1) * jnp.exp(scores)
    positive = jnp.concatenate([pos_ref[...], pack_ref[half + 1 : half + 2].astype(jnp.int32)], axis=1)
    chosen = passage_ids(stages[:-1], block, scores.shape, me_ref[0]) == positive
    sums_ref[:1] = jnp.sum(terms, axis=0, keepdims=True)
    sums_ref[1:2] = jnp.sum(jnp.where(chosen, scores, 0.0), axis=0, keepdims=True)
    sums_ref[2:] = jnp.zeros((6, scores.shape[1]), F32)
    terms_ref[...] = terms
    chosen_ref[...] = jnp.where(chosen, 1.0, 0.0)
    all_ref[...] = raw
    scales_ref[...] = scale
    part = half - rows.shape[0]
    pool_ref[:part] = jnp.concatenate([r[...] for r in early], axis=0)
    pool_ref[part:] = rows


def coef_kernel(*refs):
    q_ref, other_ref, raw_ref, scale_ref, qs_ref, terms_ref, chosen_ref, sums_ref, got_ref, dl_ref, pack_ref = refs[:11]
    kept_ref, sent_ref, qc_ref, share_ref, loss_ref, inner_ref = refs[11:]
    count = q_ref.shape[0]
    half = raw_ref.shape[0]
    sums = sums_ref[...] + jnp.concatenate([got_ref[:, count:], got_ref[:, :count]], axis=1)
    dl = jnp.concatenate([dl_ref[...], pack_ref[half : half + 1]], axis=1)
    coef = (logit_scale * dl) * (terms_ref[...] / sums[:1] - chosen_ref[...])
    pcoef = coef * qs_ref[...]
    pc = pcoef.astype(BF16)
    total = jnp.dot(pc[:, :count], q_ref[...], preferred_element_type=F32)
    total = total + jnp.dot(pc[:, count:], other_ref[...], preferred_element_type=F32)
    part = kept_ref.shape[0]
    kept_ref[...] = total[:part]
    sent_ref[...] = total[part:].astype(BF16)
    qc = wide((pcoef * scale_ref[:, :1]).astype(BF16))
    inner = jnp.sum(qc * raw_ref[...], axis=0, keepdims=True)
    qc_ref[...] = qc[:, :count].astype(BF16)
    share_ref[:half] = qc[:, count:]
    share_ref[half : half + 1] = inner[:, count:]
    share_ref[half + 1 :] = jnp.zeros((7, count), F32)
    inner_ref[...] = inner[:, :count]
    loss_ref[...] = jnp.log(sums[:1, :count]) - sums[1:2, :count]


def query_kernel(first, *refs):
    pool_ref, others_ref, qc_ref, share_ref, inner_ref, qs_ref, q_ref = refs[:7]
    out_ref, coef_ref, column_ref = refs[-3:]
    step = out_ref.shape[1]
    count = q_ref.shape[0]
    half = qc_ref.shape[0]

    @pl.when(pl.program_id(0) == 0)
    def _():
        coef_ref[:, :half] = qc_ref[...].T
        coef_ref[:, half:] = share_ref[:half].astype(BF16).T
        qs = qs_ref[:, :count]
        inner = (inner_ref[...] + share_ref[half : half + 1]) * qs * qs
        column_ref[...] = jnp.broadcast_to(inner, (128, count)).T

    at = pl.ds(pl.multiple_of((first + pl.program_id(0)) * step, step), step)
    rows = jnp.concatenate([pool_ref[:, at], others_ref[:, at]], axis=0)
    qdir = jnp.dot(coef_ref[...], rows, preferred_element_type=F32)
    out_ref[...] = (qdir - wide(q_ref[:, at]) * column_ref[:, :1]).astype(BF16)


def far_kernel(kept_ref, got_ref, *out_refs):
    total = kept_ref[...] + wide(got_ref[...])
    part = out_refs[0].shape[0]
    for k, ref in enumerate(out_refs):
        ref[...] = total[k * part : (k + 1) * part].astype(ref.dtype)


def passage_kernel(n, p_ref, total_ref, *refs):
    out_ref = refs[n]
    pdir = total_ref[...]
    for r in refs[:n]:
        pdir = pdir + wide(r[...])
    f = wide(p_ref[...])
    scale = lax.rsqrt(jnp.sum(f * f, axis=1, keepdims=True) + norm_eps)
    unit = f * scale
    inner = jnp.sum(unit * pdir, axis=1, keepdims=True)
    out_ref[...] = (scale * (pdir - unit * inner)).astype(BF16)


def make_local(loop, narrow):
    stages = stage_masks(loop)

    def body(queries, passages, pos_ids, neg_ids, neg_mask, neg_counts, d_loss):
        me = lax.axis_index("loop").astype(jnp.int32).reshape(1)
        block, width = passages.shape
        count, slots = neg_ids.shape
        half = loop * block // 2
        core = stages[-1][1]

        def cross(x, mask):
            return swap(x, "loop", loop, mask)

        first = [passages] + [cross(passages, m) for m in stages[0][1:]]
        pool = [jnp.concatenate(first[k : k + 2], axis=0) for k in (0, 2)]
        for _, m in stages[1:-2]:
            pool = [jnp.concatenate(pool + [cross(t, m) for t in pool], axis=0)]
        pool = pool + [cross(t, stages[-2][1]) for t in pool]
        n = len(pool)

        others = cross(queries, core)
        row = lambda x: x.reshape(1, count)
        weights, pack = call(
            functools.partial(weight_kernel, stages, block),
            [((half, count), F32), ((half + 8, count), F32)],
            (me, neg_ids.T, neg_mask.T, row(neg_counts), row(pos_ids), row(d_loss), queries),
            in_specs=[SMEM] + [HBM] * 6,
            limit=WIDE_LIMIT,
            flops=10000000,
            scratch_shapes=[pltpu.VMEM((slots, count), jnp.int32)] * 2
            + [pltpu.VMEM((1, count), jnp.int32)] * 2
            + [pltpu.VMEM((1, count), F32), pltpu.SemaphoreType.DMA((5,))],
        )
        pack = cross(pack, core)

        both = 2 * count
        raw, scale, qs = call(
            functools.partial(early_kernel, n // 2),
            [((half // 2, both), F32), ((half // 2, 128), F32), ((1, both), F32)],
            (*pool[: n // 2], queries, others),
            flops=2 * half * count * width,
        )
        rows, raw, scale, terms, chosen, sums = call(
            functools.partial(late_kernel, n, stages, block),
            [((half, width), BF16), ((half, both), F32), ((half, 128), F32)] + [((half, both), F32)] * 2 + [((8, both), F32)],
            (me, *pool, queries, others, raw, scale, qs, weights, pack, row(pos_ids)),
            in_specs=[SMEM] + [VMEM] * (n + 8),
            flops=2 * half * count * width,
        )
        kept, sent, qc, share, loss, inner = call(
            coef_kernel,
            [((half // 2, width), F32), ((half // 2, width), BF16), ((half, count), BF16), ((half + 8, count), F32)]
            + [((1, count), F32)] * 2,
            (queries, others, raw, scale, qs, terms, chosen, sums, cross(sums, core), row(d_loss), pack),
            flops=4 * half * count * width,
        )

        got = cross(sent, stages[-2][1])
        for _, m in stages[1:-2][::-1]:
            total = kept + wide(got)
            part = total.shape[0] // 2
            kept, got = total[:part], cross(total[part:].astype(BF16), m)
        term = (block, width)
        total, *terms = call(far_kernel, [(term, F32)] + [(term, BF16)] * 3, (kept, got))
        moved = [cross(terms[k - 1], stages[0][k]) for k in (3, 2, 1)]
        for t in moved:
            total = total + wide(t)
        moved = []
        for b in range(narrow.bit_length() - 1):
            if moved:
                total = total + wide(moved.pop())
            moved.append(swap(total.astype(BF16), "narrow", narrow, 1 << b))

        step = 512
        calls = 2
        steps = width // step // calls
        grad_queries = []
        operands = (rows, cross(rows, core), qc, cross(share, core), inner, qs, queries)
        for k in range(calls):
            grad_queries = call(
                functools.partial(query_kernel, k * steps),
                [(queries.shape, BF16)],
                (*operands, *grad_queries),
                grid=(steps,),
                in_specs=[VMEM] * 7 + [pl.BlockSpec(memory_space=pl.ANY)] * len(grad_queries),
                out_specs=(pl.BlockSpec((count, step), lambda i, k=k: (0, i + k * steps)),),
                input_output_aliases={7: 0} if grad_queries else {},
                scratch_shapes=[pltpu.VMEM((count, 2 * half), BF16), pltpu.VMEM((count, 128), F32)],
                flops=4 * half * count * width // calls,
                moved=3000000,
            )
        (grad_passages,) = call(
            functools.partial(passage_kernel, len(moved)), [(passages.shape, BF16)], (passages, total, *moved)
        )
        return loss.reshape(count), *grad_queries, grad_passages

    return body


def solution(mesh):
    both = ("loop", "narrow")
    return jax.shard_map(
        make_local(mesh.shape["loop"], mesh.shape["narrow"]),
        mesh=mesh,
        in_specs=(P(both, None), P("loop", None), P(both), P(both, None), P(both, None), P(both), P(both)),
        out_specs=(P(both), P(both, None), P("loop", None)),
        check_vma=False,
    )
```

time: 165 us -> 47.1 us (0.29)
  waiting for transfers between devices: 107 us -> 13.9 us
  blocking collectives: 24.6 us -> 0 us
  Pallas kernels: 0 us -> 15.7 us
  starting transfers between devices: 0.08 us -> 15.5 us
  between operations: 14.8 us -> 0.74 us
  other arithmetic: 11.5 us -> 0.87 us
  matrix products: 3.43 us -> 0 us
  local copies, waits for them, and re-layouts: 3.01 us -> 0.03 us
    unnamed x3 -> x0, waiting for transfers between devices: 86.6 us -> none
    all_gather x1 -> x0, blocking collectives: 24.6 us -> none  [local(): pool = lax.all_gather(pnorm, 'loop', axis=0, tiled=True)]
    psum x1 -> x0, waiting for transfers between devices: 20.2 us -> none  [local(): pdir = lax.psum(partial_dir, 'narrow')]
    pallas_call x0 -> x8, Pallas kernels: none -> 15.7 us  [call(): pl.pallas_call(kernel, out_shape=tuple((jax.ShapeDtypeStruct(*out) for ou...]
    ppermute x0 -> x15, starting transfers between devices: none -> 15.5 us  [swap(): return lax.ppermute(x, axis, [(i, i ^ mask) for i in range(size)])]
    ppermute x0 -> x15, waiting for transfers between devices: none -> 13.9 us  [swap(): return lax.ppermute(x, axis, [(i, i ^ mask) for i in range(size)])]
    reduce_sum x5 -> x0, other arithmetic: 4.58 us -> none  [the longest x2 3.13 us: normalize(): scales = lax.rsqrt(jnp.sum(wide * wide, axis=-1) + norm_eps)]
    convert_element_type x2 -> x1, other arithmetic: 4.01 us -> 0.04 us  [body(): moved.append(swap(total.astype(BF16), 'narrow', narrow, 1 << b))]
  transfers between devices with their start and end apart: 2 -> 15, of which waited for: 2 -> 7; matrix products, arithmetic and copies ran while one was open for 3% -> 2% of each run, Pallas kernels for 0% -> 11%
where the time goes in v1:
time: 47.1 us; the launch traced here: 46.8 us
  Pallas kernels  15.7 us (33%)
  starting transfers between devices  15.5 us (33%)
  waiting for transfers between devices  13.9 us (30%)
  other arithmetic  0.87 us (2%)
  between operations  0.74 us (2%)
    pallas_call x8, Pallas kernels, call(): pl.pallas_call(kernel, out_shape=tuple((jax.ShapeDtypeStruct(*out) for ou...  15.7 us
    ppermute x15, starting transfers between devices, swap(): return lax.ppermute(x, axis, [(i, i ^ mask) for i in range(size)])  15.5 us
    ppermute x15, waiting for transfers between devices, swap(): return lax.ppermute(x, axis, [(i, i ^ mask) for i in range(size)])  13.9 us
  transfers between devices with their start and end apart: 15, of which 7 were waited for; matrix products, arithmetic and copies ran while one was open for 2% of the time, Pallas kernels for 11%

profile of v1, /device:TPU:0, one launch (start us, length us, event | category | flops | bytes accessed | tf_op | source)
XLA Modules:
  0.0 46.8 jit_solution(2231826265286308537)
XLA Ops:
  0.6 0.0 copy-start
  0.6 0.6 %collective-permute-start = (bf16[256,4096]{1,0:T(8,128)(2,1)}, bf16[256,4096]{1,0:T(8,128)(2,1)}, u32[]{:S(2)}, u32[]{:S(2)}) collective-permute-start(bf16[256,4096]{1,0:T(8,128)(2,1)} %refs_6_.3), channel_id=1, source_target_pairs={{0,2},{2,0},{4,6},{6,4},{8,10},{10,8},{12,14},{14,12},{16,18},{18,... | collective-permute-start | bytes 6291464 | tf_op jit(solution)/shard_map/ppermute | solution.py:32
  1.2 3.7 %collective-permute-start.2 = (bf16[4,4096]{1,0:T(4,128)(2,1)}, bf16[4,4096]{1,0:T(4,128)(2,1)S(1)}, u32[]{:S(2)}, u32[]{:S(2)}) collective-permute-start(bf16[4,4096]{1,0:T(4,128)(2,1)} %p_ref.1), channel_id=1, source_target_pairs={{0,18},{2,16},{4,22},{6,20},{8,26},{10,24},{12,30},{14,28},{16,2},... | collective-permute-start | bytes 98312 | tf_op jit(solution)/shard_map/ppermute | solution.py:32
  4.9 1.0 %collective-permute-start.3 = (bf16[4,4096]{1,0:T(4,128)(2,1)}, bf16[4,4096]{1,0:T(4,128)(2,1)S(1)}, u32[]{:S(2)}, u32[]{:S(2)}) collective-permute-start(bf16[4,4096]{1,0:T(4,128)(2,1)} %p_ref.1), channel_id=1, source_target_pairs={{0,26},{2,24},{4,30},{6,28},{8,18},{10,16},{12,22},{14,20},{16,10}... | collective-permute-start | bytes 98312 | tf_op jit(solution)/shard_map/ppermute | solution.py:32
  5.9 0.2 collective-permute-start.1
  6.2 0.6 %collective-permute-done.2 = bf16[4,4096]{1,0:T(4,128)(2,1)S(1)} collective-permute-done((bf16[4,4096]{1,0:T(4,128)(2,1)}, bf16[4,4096]{1,0:T(4,128)(2,1)S(1)}, u32[]{:S(2)}, u32[]{:S(2)}) %collective-permute-start.2) | collective-permute-done | bytes 32800 | tf_op jit(solution)/shard_map/ppermute | solution.py:32
  6.8 3.6 %collective-permute-done.3 = bf16[4,4096]{1,0:T(4,128)(2,1)S(1)} collective-permute-done((bf16[4,4096]{1,0:T(4,128)(2,1)}, bf16[4,4096]{1,0:T(4,128)(2,1)S(1)}, u32[]{:S(2)}, u32[]{:S(2)}) %collective-permute-start.3) | collective-permute-done | bytes 32800 | tf_op jit(solution)/shard_map/ppermute | solution.py:32
  10.5 1.4 %collective-permute-start.5 = (bf16[8,4096]{1,0:T(8,128)(2,1)S(1)}, bf16[8,4096]{1,0:T(8,128)(2,1)S(1)}, u32[]{:S(2)}, u32[]{:S(2)}) collective-permute-start(bf16[8,4096]{1,0:T(8,128)(2,1)S(1)} %pad_maximum_fusion.1.refs_1_), channel_id=1, source_target_pairs={{0,6},{2,4},{4,2},{6,0},{8,14},{10,12},{12,10},{14,8},{16,22},{18,... | collective-permute-start | bytes 196616 | tf_op jit(solution)/shard_map/ppermute | solution.py:32
  11.9 0.0 collective-permute-done.1
  11.9 0.8 %pad_maximum_fusion.refs_0_ = bf16[8,4096]{1,0:T(8,128)(2,1)S(1)} fusion(bf16[4,4096]{1,0:T(4,128)(2,1)S(1)} %collective-permute-done.1, bf16[4,4096]{1,0:T(4,128)(2,1)} %p_ref.1), kind=kLoop, calls=%fused_computation | loop fusion | flops 131072 | bytes 131072 | tf_op jit(solution)/shard_map/concatenate | solution.py:213
  12.7 0.4 collective-permute-start.4
  13.1 1.7 %shard_map.95 = (f32[32,256]{1,0:T(8,128)}, f32[40,256]{1,0:T(8,128)}) custom-call(s32[1]{0:T(128)} %bitcast.me_ref, s32[32,256]{1,0:T(8,128)} %bitcast.11, s32[32,256]{1,0:T(8,128)} %bitcast.12, s32[1,256]{1,0:T(1,128)} %bitcast.13, s32[1,256]{1,0:T(1,128)} %bitcast.7, f32[1,256]{1,0:T(1,128)} %bitcast.9, bf16[256,4096]{1,0:T(8,128)(2,1)} %refs_6_.3), custom_call_target="tpu_custom_call" | custom-call | flops 10000000 | bytes 1000000 | tf_op jit(solution)/shard_map/pallas_call | solution.py:41
  14.8 0.0 copy-start.2
  14.8 0.0 copy-start.3
  14.8 0.3 collective-permute-start.6
  15.2 0.0 collective-permute-done.refs_3_.refs_5_.refs_1_
  15.2 0.0 copy-done
  15.2 2.8 %shard_map.94 = (f32[16,512]{1,0:T(8,128)S(1)}, f32[16,128]{1,0:T(8,128)S(1)}, f32[1,512]{1,0:T(1,128)S(1)}) custom-call(bf16[8,4096]{1,0:T(8,128)(2,1)S(1)} %pad_maximum_fusion.refs_0_, bf16[8,4096]{1,0:T(8,128)(2,1)S(1)} %pad_maximum_fusion.1.refs_1_, bf16[256,4096]{1,0:T(8,128)(2,1)S(1)} %copy-done, ...), custom_call_target="tpu_custom_call" | custom-call | flops 67108864 | bytes 1000000 | tf_op jit(solution)/shard_map/pallas_call | solution.py:41
  17.9 0.0 collective-permute-done.6.refs_10_
  17.9 0.0 collective-permute-done.5.refs_3_
  18.0 0.0 collective-permute-done.4.refs_2_
  18.0 0.0 copy-done.2
  18.0 0.0 copy-done.3
  18.0 0.0 copy-start.4
  18.0 2.8 %shard_map.96 = (bf16[32,4096]{1,0:T(8,128)(2,1)S(1)}, f32[32,512]{1,0:T(8,128)S(1)}, f32[32,128]{1,0:T(8,128)S(1)}, f32[32,512]{1,0:T(8,128)S(1)}, f32[32,512]{1,0:T(8,128)S(1)}, /*index=5*/f32[8,512]{1,0:T(8,128)S(1)}) custom-call(s32[1]{0:T(128)} %bitcast.me_ref, bf16[8,4096]{1,0:T(8,128)(2,1)S(1)} %pad_maximum_fusion.refs_0_, ...), custom_call_target="tpu_custom_call" | custom-call | flops 67108864 | bytes 1000000 | tf_op jit(solution)/shard_map/pallas_call | solution.py:41
  20.8 0.3 collective-permute-start.7
  21.2 0.9 %collective-permute-done.7.refs_8_ = f32[8,512]{1,0:T(8,128)S(1)} collective-permute-done((f32[8,512]{1,0:T(8,128)S(1)}, f32[8,512]{1,0:T(8,128)S(1)}, u32[]{:S(2)}, u32[]{:S(2)}) %collective-permute-start.7) | collective-permute-done | bytes 16416 | tf_op jit(solution)/shard_map/ppermute | solution.py:32
  22.1 0.0 copy-done.4
  22.1 0.0 copy-start.1
  22.1 2.9 %shard_map.97 = (f32[16,4096]{1,0:T(8,128)S(1)}, bf16[16,4096]{1,0:T(8,128)(2,1)S(1)}, bf16[32,256]{1,0:T(8,128)(2,1)S(1)}, f32[40,256]{1,0:T(8,128)S(1)}, f32[1,256]{1,0:T(1,128)}, /*index=5*/f32[1,256]{1,0:T(1,128)S(1)}) custom-call(bf16[256,4096]{1,0:T(8,128)(2,1)S(1)} %copy-done, bf16[256,4096]{1,0:T(8,128)(2,1)} %collective-permute-done.refs_3_.refs_5_.refs_1_, ...), custom_call_target="tpu_custom_call" | custom-call | flops 134217728 | bytes 1000000 | tf_op jit(solution)/shard_map/pallas_call | solution.py:41
  25.0 1.4 %collective-permute-start.10 = (bf16[16,4096]{1,0:T(8,128)(2,1)S(1)}, bf16[16,4096]{1,0:T(8,128)(2,1)S(1)}, u32[]{:S(2)}, u32[]{:S(2)}) collective-permute-start(bf16[16,4096]{1,0:T(8,128)(2,1)S(1)} %get-tuple-element.40), channel_id=1, source_target_pairs={{0,6},{2,4},{4,2},{6,0},{8,14},{10,12},{12,10},{14,8},{16,22},{18,... | collective-permute-start | bytes 393224 | tf_op jit(solution)/shard_map/ppermute | solution.py:32
  26.4 3.9 %collective-permute-done.10.got_ref = bf16[16,4096]{1,0:T(8,128)(2,1)S(1)} collective-permute-done((bf16[16,4096]{1,0:T(8,128)(2,1)S(1)}, bf16[16,4096]{1,0:T(8,128)(2,1)S(1)}, u32[]{:S(2)}, u32[]{:S(2)}) %collective-permute-start.10) | collective-permute-done | bytes 131104 | tf_op jit(solution)/shard_map/ppermute | solution.py:32
  30.4 1.7 %collective-permute-start.11 = (bf16[4,4096]{1,0:T(4,128)(2,1)S(1)}, bf16[4,4096]{1,0:T(4,128)(2,1)S(1)}, u32[]{:S(2)}, u32[]{:S(2)}) collective-permute-start(bf16[4,4096]{1,0:T(4,128)(2,1)S(1)} %get-tuple-element.42), channel_id=1, source_target_pairs={{0,26},{2,24},{4,30},{6,28},{8,18},{10,16},{12,22},{14,20},{16,10}... | collective-permute-start | bytes 98312 | tf_op jit(solution)/shard_map/ppermute | solution.py:32
  32.1 0.0 collective-permute-start.12
  32.1 2.4 %collective-permute-start.13 = (bf16[4,4096]{1,0:T(4,128)(2,1)S(1)}, bf16[4,4096]{1,0:T(4,128)(2,1)S(1)}, u32[]{:S(2)}, u32[]{:S(2)}) collective-permute-start(bf16[4,4096]{1,0:T(4,128)(2,1)S(1)} %get-tuple-element.44), channel_id=1, source_target_pairs={{0,10},{2,8},{4,14},{6,12},{8,2},{10,0},{12,6},{14,4},{16,26},{18,... | collective-permute-start | bytes 98312 | tf_op jit(solution)/shard_map/ppermute | solution.py:32
  34.5 0.2 collective-permute-start.8
  34.7 0.3 collective-permute-start.9
  35.0 0.6 %collective-permute-done.11 = bf16[4,4096]{1,0:T(4,128)(2,1)S(1)} collective-permute-done((bf16[4,4096]{1,0:T(4,128)(2,1)S(1)}, bf16[4,4096]{1,0:T(4,128)(2,1)S(1)}, u32[]{:S(2)}, u32[]{:S(2)}) %collective-permute-start.11) | collective-permute-done | bytes 32800 | tf_op jit(solution)/shard_map/ppermute | solution.py:32
  35.6 1.7 %collective-permute-done.12 = bf16[4,4096]{1,0:T(4,128)(2,1)S(1)} collective-permute-done((bf16[4,4096]{1,0:T(4,128)(2,1)S(1)}, bf16[4,4096]{1,0:T(4,128)(2,1)S(1)}, u32[]{:S(2)}, u32[]{:S(2)}) %collective-permute-start.12) | collective-permute-done | bytes 32800 | tf_op jit(solution)/shard_map/ppermute | solution.py:32
  37.3 0.0 collective-permute-done.13
  37.4 1.6 %collective-permute-start.14 = (bf16[4,4096]{1,0:T(4,128)(2,1)S(1)}, bf16[4,4096]{1,0:T(4,128)(2,1)S(1)}, u32[]{:S(2)}, u32[]{:S(2)}) collective-permute-start(bf16[4,4096]{1,0:T(4,128)(2,1)S(1)} %get-tuple-element.45), channel_id=1, source_target_pairs={{0,1},{1,0},{2,3},{3,2},{4,5},{5,4},{6,7},{7,6},{8,9},{9,8},{10,11... | collective-permute-start | bytes 98312 | tf_op jit(solution)/shard_map/ppermute | solution.py:32
  38.9 2.4 %collective-permute-done.14.refs_0_ = bf16[4,4096]{1,0:T(4,128)(2,1)S(1)} collective-permute-done((bf16[4,4096]{1,0:T(4,128)(2,1)S(1)}, bf16[4,4096]{1,0:T(4,128)(2,1)S(1)}, u32[]{:S(2)}, u32[]{:S(2)}) %collective-permute-start.14) | collective-permute-done | bytes 32800 | tf_op jit(solution)/shard_map/ppermute | solution.py:32
  41.3 0.0 copy-done.1
  41.3 0.9 %shard_map.101 = bf16[4,4096]{1,0:T(4,128)(2,1)} custom-call(bf16[4,4096]{1,0:T(4,128)(2,1)S(1)} %copy-done.1, f32[4,4096]{1,0:T(4,128)S(1)} %get-tuple-element.46.total_ref, bf16[4,4096]{1,0:T(4,128)(2,1)S(1)} %collective-permute-done.14.refs_0_), custom_call_target="tpu_custom_call" | custom-call | flops 200000 | bytes 1000000 | tf_op jit(solution)/shard_map/pallas_call | solution.py:41
  42.2 0.0 collective-permute-done.9.refs_3_
  42.2 0.0 collective-permute-done.8.refs_1_
  42.2 2.3 %shard_map.98.refs_7_ = bf16[256,4096]{1,0:T(8,128)(2,1)} custom-call(bf16[32,4096]{1,0:T(8,128)(2,1)S(1)} %get-tuple-element.35.refs_0_, bf16[32,4096]{1,0:T(8,128)(2,1)S(1)} %collective-permute-done.8.refs_1_, bf16[32,256]{1,0:T(8,128)(2,1)S(1)} %get-tuple-element.36.refs_2_, f32[40,256]{1,0:T(8,128)S(1)} %collective-permute-done.9.refs_3_, ...), custom_call_target="tpu_custom_call" | custom-call | flops 67108864 | bytes 3000000 | tf_op jit(solution)/shard_map/pallas_call | solution.py:41
  44.5 2.3 %shard_map.99 = bf16[256,4096]{1,0:T(8,128)(2,1)} custom-call(bf16[32,4096]{1,0:T(8,128)(2,1)S(1)} %get-tuple-element.35.refs_0_, bf16[32,4096]{1,0:T(8,128)(2,1)S(1)} %collective-permute-done.8.refs_1_, bf16[32,256]{1,0:T(8,128)(2,1)S(1)} %get-tuple-element.36.refs_2_, ...), custom_call_target="tpu_custom_call", output_to_operand_aliasing={{}: (7, {})} | custom-call | flops 67108864 | bytes 3000000 | tf_op jit(solution)/shard_map/pallas_call | solution.py:41
  (3 shorter events, 0.1 us)
Async XLA Ops:
  0.6 14.5 %copy-start = (bf16[256,4096]{1,0:T(8,128)(2,1)S(1)}, bf16[256,4096]{1,0:T(8,128)(2,1)}, u32[]{:S(2)}) copy-start(bf16[256,4096]{1,0:T(8,128)(2,1)} %refs_6_.3) | copy-start | bytes 6291460
  0.6 14.5 %collective-permute-start = (bf16[256,4096]{1,0:T(8,128)(2,1)}, bf16[256,4096]{1,0:T(8,128)(2,1)}, u32[]{:S(2)}, u32[]{:S(2)}) collective-permute-start(bf16[256,4096]{1,0:T(8,128)(2,1)} %refs_6_.3), channel_id=1, source_target_pairs={{0,2},{2,0},{4,6},{6,4},{8,10},{10,8},{12,14},{14,12},{16,18},{18,... | collective-permute-start | bytes 6291464 | tf_op jit(solution)/shard_map/ppermute | solution.py:32
  1.2 5.6 %collective-permute-start.2 = (bf16[4,4096]{1,0:T(4,128)(2,1)}, bf16[4,4096]{1,0:T(4,128)(2,1)S(1)}, u32[]{:S(2)}, u32[]{:S(2)}) collective-permute-start(bf16[4,4096]{1,0:T(4,128)(2,1)} %p_ref.1), channel_id=1, source_target_pairs={{0,18},{2,16},{4,22},{6,20},{8,26},{10,24},{12,30},{14,28},{16,2},... | collective-permute-start | bytes 98312 | tf_op jit(solution)/shard_map/ppermute | solution.py:32
  4.9 5.5 %collective-permute-start.3 = (bf16[4,4096]{1,0:T(4,128)(2,1)}, bf16[4,4096]{1,0:T(4,128)(2,1)S(1)}, u32[]{:S(2)}, u32[]{:S(2)}) collective-permute-start(bf16[4,4096]{1,0:T(4,128)(2,1)} %p_ref.1), channel_id=1, source_target_pairs={{0,26},{2,24},{4,30},{6,28},{8,18},{10,16},{12,22},{14,20},{16,10}... | collective-permute-start | bytes 98312 | tf_op jit(solution)/shard_map/ppermute | solution.py:32
  5.9 6.0 %collective-permute-start.1 = (bf16[4,4096]{1,0:T(4,128)(2,1)}, bf16[4,4096]{1,0:T(4,128)(2,1)S(1)}, u32[]{:S(2)}, u32[]{:S(2)}) collective-permute-start(bf16[4,4096]{1,0:T(4,128)(2,1)} %p_ref.1), channel_id=1, source_target_pairs={{0,10},{2,8},{4,14},{6,12},{8,2},{10,0},{12,6},{14,4},{16,26},{18,... | collective-permute-start | bytes 98312 | tf_op jit(solution)/shard_map/ppermute | solution.py:32
  10.5 7.5 %collective-permute-start.5 = (bf16[8,4096]{1,0:T(8,128)(2,1)S(1)}, bf16[8,4096]{1,0:T(8,128)(2,1)S(1)}, u32[]{:S(2)}, u32[]{:S(2)}) collective-permute-start(bf16[8,4096]{1,0:T(8,128)(2,1)S(1)} %pad_maximum_fusion.1.refs_1_), channel_id=1, source_target_pairs={{0,6},{2,4},{4,2},{6,0},{8,14},{10,12},{12,10},{14,8},{16,22},{18,... | collective-permute-start | bytes 196616 | tf_op jit(solution)/shard_map/ppermute | solution.py:32
  12.7 5.3 %collective-permute-start.4 = (bf16[8,4096]{1,0:T(8,128)(2,1)S(1)}, bf16[8,4096]{1,0:T(8,128)(2,1)S(1)}, u32[]{:S(2)}, u32[]{:S(2)}) collective-permute-start(bf16[8,4096]{1,0:T(8,128)(2,1)S(1)} %pad_maximum_fusion.refs_0_), channel_id=1, source_target_pairs={{0,6},{2,4},{4,2},{6,0},{8,14},{10,12},{12,10},{14,8},{16,22},{18,... | collective-permute-start | bytes 196616 | tf_op jit(solution)/shard_map/ppermute | solution.py:32
  14.8 3.2 %copy-start.2 = (f32[32,256]{1,0:T(8,128)S(1)}, f32[32,256]{1,0:T(8,128)}, u32[]{:S(2)}) copy-start(f32[32,256]{1,0:T(8,128)} %get-tuple-element.27.refs_9_) | copy-start | bytes 98308
  14.8 3.1 %copy-start.3 = (s32[256]{0:T(256)S(1)}, s32[256]{0:T(256)}, u32[]{:S(2)}) copy-start(s32[256]{0:T(256)} %param.9) | copy-start | bytes 3076
  14.8 3.1 %collective-permute-start.6 = (f32[40,256]{1,0:T(8,128)}, f32[40,256]{1,0:T(8,128)S(1)}, u32[]{:S(2)}, u32[]{:S(2)}) collective-permute-start(f32[40,256]{1,0:T(8,128)} %get-tuple-element.28), channel_id=1, source_target_pairs={{0,2},{2,0},{4,6},{6,4},{8,10},{10,8},{12,14},{14,12},{16,18},{18,... | collective-permute-start | bytes 122888 | tf_op jit(solution)/shard_map/ppermute | solution.py:32
  18.0 4.1 %copy-start.4 = (f32[256]{0:T(256)S(1)}, f32[256]{0:T(256)}, u32[]{:S(2)}) copy-start(f32[256]{0:T(256)} %param.13) | copy-start | bytes 3076
  20.8 1.2 %collective-permute-start.7 = (f32[8,512]{1,0:T(8,128)S(1)}, f32[8,512]{1,0:T(8,128)S(1)}, u32[]{:S(2)}, u32[]{:S(2)}) collective-permute-start(f32[8,512]{1,0:T(8,128)S(1)} %get-tuple-element.33.refs_7_), channel_id=1, source_target_pairs={{0,2},{2,0},{4,6},{6,4},{8,10},{10,8},{12,14},{14,12},{16,18},{18,... | collective-permute-start | bytes 49160 | tf_op jit(solution)/shard_map/ppermute | solution.py:32
  22.1 19.2 %copy-start.1 = (bf16[4,4096]{1,0:T(4,128)(2,1)S(1)}, bf16[4,4096]{1,0:T(4,128)(2,1)}, u32[]{:S(2)}) copy-start(bf16[4,4096]{1,0:T(4,128)(2,1)} %p_ref.1) | copy-start | bytes 98308
  25.0 5.3 %collective-permute-start.10 = (bf16[16,4096]{1,0:T(8,128)(2,1)S(1)}, bf16[16,4096]{1,0:T(8,128)(2,1)S(1)}, u32[]{:S(2)}, u32[]{:S(2)}) collective-permute-start(bf16[16,4096]{1,0:T(8,128)(2,1)S(1)} %get-tuple-element.40), channel_id=1, source_target_pairs={{0,6},{2,4},{4,2},{6,0},{8,14},{10,12},{12,10},{14,8},{16,22},{18,... | collective-permute-start | bytes 393224 | tf_op jit(solution)/shard_map/ppermute | solution.py:32
  30.4 5.2 %collective-permute-start.11 = (bf16[4,4096]{1,0:T(4,128)(2,1)S(1)}, bf16[4,4096]{1,0:T(4,128)(2,1)S(1)}, u32[]{:S(2)}, u32[]{:S(2)}) collective-permute-start(bf16[4,4096]{1,0:T(4,128)(2,1)S(1)} %get-tuple-element.42), channel_id=1, source_target_pairs={{0,26},{2,24},{4,30},{6,28},{8,18},{10,16},{12,22},{14,20},{16,10}... | collective-permute-start | bytes 98312 | tf_op jit(solution)/shard_map/ppermute | solution.py:32
  32.1 5.2 %collective-permute-start.12 = (bf16[4,4096]{1,0:T(4,128)(2,1)S(1)}, bf16[4,4096]{1,0:T(4,128)(2,1)S(1)}, u32[]{:S(2)}, u32[]{:S(2)}) collective-permute-start(bf16[4,4096]{1,0:T(4,128)(2,1)S(1)} %get-tuple-element.43), channel_id=1, source_target_pairs={{0,18},{2,16},{4,22},{6,20},{8,26},{10,24},{12,30},{14,28},{16,2},... | collective-permute-start | bytes 98312 | tf_op jit(solution)/shard_map/ppermute | solution.py:32
  32.1 5.2 %collective-permute-start.13 = (bf16[4,4096]{1,0:T(4,128)(2,1)S(1)}, bf16[4,4096]{1,0:T(4,128)(2,1)S(1)}, u32[]{:S(2)}, u32[]{:S(2)}) collective-permute-start(bf16[4,4096]{1,0:T(4,128)(2,1)S(1)} %get-tuple-element.44), channel_id=1, source_target_pairs={{0,10},{2,8},{4,14},{6,12},{8,2},{10,0},{12,6},{14,4},{16,26},{18,... | collective-permute-start | bytes 98312 | tf_op jit(solution)/shard_map/ppermute | solution.py:32
  34.5 7.8 %collective-permute-start.8 = (bf16[32,4096]{1,0:T(8,128)(2,1)S(1)}, bf16[32,4096]{1,0:T(8,128)(2,1)S(1)}, u32[]{:S(2)}, u32[]{:S(2)}) collective-permute-start(bf16[32,4096]{1,0:T(8,128)(2,1)S(1)} %get-tuple-element.35.refs_0_), channel_id=1, source_target_pairs={{0,2},{2,0},{4,6},{6,4},{8,10},{10,8},{12,14},{14,12},{16,18},{18,... | collective-permute-start | bytes 786440 | tf_op jit(solution)/shard_map/ppermute | solution.py:32
  34.7 7.5 %collective-permute-start.9 = (f32[40,256]{1,0:T(8,128)S(1)}, f32[40,256]{1,0:T(8,128)S(1)}, u32[]{:S(2)}, u32[]{:S(2)}) collective-permute-start(f32[40,256]{1,0:T(8,128)S(1)} %get-tuple-element.37), channel_id=1, source_target_pairs={{0,2},{2,0},{4,6},{6,4},{8,10},{10,8},{12,14},{14,12},{16,18},{18,... | collective-permute-start | bytes 122888 | tf_op jit(solution)/shard_map/ppermute | solution.py:32
  37.4 4.0 %collective-permute-start.14 = (bf16[4,4096]{1,0:T(4,128)(2,1)S(1)}, bf16[4,4096]{1,0:T(4,128)(2,1)S(1)}, u32[]{:S(2)}, u32[]{:S(2)}) collective-permute-start(bf16[4,4096]{1,0:T(4,128)(2,1)S(1)} %get-tuple-element.45), channel_id=1, source_target_pairs={{0,1},{1,0},{2,3},{3,2},{4,5},{5,4},{6,7},{7,6},{8,9},{9,8},{10,11... | collective-permute-start | bytes 98312 | tf_op jit(solution)/shard_map/ppermute | solution.py:32

commit v2 on v1

--- a/solution.py
+++ b/solution.py
@@ -48,18 +48,23 @@
     )(*args)
 
 
+def split_index(x, n):
+    if n & (n - 1):
+        return x // n, x % n
+    return x >> (n.bit_length() - 1), x & (n - 1)
+
+
 def passage_ids(stages, block, shape, me):
     row = lax.broadcasted_iota(jnp.int32, shape, 0)
-    place = row // block
-    digits, owner = place, jnp.full(shape, me, jnp.int32)
+    digits, inside = split_index(row, block)
+    owner = jnp.full(shape, me, jnp.int32)
     for masks in stages:
-        digit = digits % len(masks)
-        digits = digits // len(masks)
+        digits, digit = split_index(digits, len(masks))
         chosen = jnp.zeros(shape, jnp.int32)
         for k, m in enumerate(masks[1:]):
             chosen = jnp.where(digit == k + 1, m, chosen)
         owner = owner ^ chosen
-    return owner * block + (row - place * block)
+    return owner * block + inside
 
 
 def weight_kernel(stages, block, me_ref, *refs):
@@ -131,29 +136,46 @@
     pool_ref[part:] = rows
 
 
+def direction_terms(pcoef, columns, q_ref, other_ref, kept_ref, sent_ref):
+    count = q_ref.shape[0]
+    pc = pcoef.astype(BF16)
+    total = jnp.dot(pc[:, :count], q_ref[:, columns], preferred_element_type=F32)
+    total = total + jnp.dot(pc[:, count:], other_ref[:, columns], preferred_element_type=F32)
+    part = kept_ref.shape[0]
+    kept_ref[...] = total[:part]
+    sent_ref[...] = total[part:].astype(BF16)
+
+
 def coef_kernel(*refs):
-    q_ref, other_ref, raw_ref, scale_ref, qs_ref, terms_ref, chosen_ref, sums_ref, got_ref, dl_ref, pack_ref = refs[:11]
-    kept_ref, sent_ref, qc_ref, share_ref, loss_ref, inner_ref = refs[11:]
+    q_ref, other_ref, qs_ref, terms_ref, chosen_ref, sums_ref, got_ref, dl_ref, pack_ref = refs[:9]
+    kept_ref, sent_ref, coef_ref, all_ref = refs[9:]
     count = q_ref.shape[0]
-    half = raw_ref.shape[0]
+    half = terms_ref.shape[0]
     sums = sums_ref[...] + jnp.concatenate([got_ref[:, count:], got_ref[:, :count]], axis=1)
     dl = jnp.concatenate([dl_ref[...], pack_ref[half : half + 1]], axis=1)
     coef = (logit_scale * dl) * (terms_ref[...] / sums[:1] - chosen_ref[...])
     pcoef = coef * qs_ref[...]
-    pc = pcoef.astype(BF16)
-    total = jnp.dot(pc[:, :count], q_ref[...], preferred_element_type=F32)
-    total = total + jnp.dot(pc[:, count:], other_ref[...], preferred_element_type=F32)
-    part = kept_ref.shape[0]
-    kept_ref[...] = total[:part]
-    sent_ref[...] = total[part:].astype(BF16)
-    qc = wide((pcoef * scale_ref[:, :1]).astype(BF16))
+    direction_terms(pcoef, slice(0, kept_ref.shape[1]), q_ref, other_ref, kept_ref, sent_ref)
+    coef_ref[...] = pcoef
+    all_ref[...] = sums
+
+
+def other_columns_kernel(q_ref, other_ref, coef_ref, kept_ref, sent_ref):
+    width = q_ref.shape[1]
+    direction_terms(coef_ref[...], slice(width - kept_ref.shape[1], width), q_ref, other_ref, kept_ref, sent_ref)
+
+
+def share_kernel(raw_ref, scale_ref, coef_ref, sums_ref, qc_ref, share_ref, loss_ref, inner_ref):
+    half = raw_ref.shape[0]
+    count = qc_ref.shape[1]
+    qc = wide((coef_ref[...] * scale_ref[:, :1]).astype(BF16))
     inner = jnp.sum(qc * raw_ref[...], axis=0, keepdims=True)
     qc_ref[...] = qc[:, :count].astype(BF16)
     share_ref[:half] = qc[:, count:]
     share_ref[half : half + 1] = inner[:, count:]
     share_ref[half + 1 :] = jnp.zeros((7, count), F32)
     inner_ref[...] = inner[:, :count]
-    loss_ref[...] = jnp.log(sums[:1, :count]) - sums[1:2, :count]
+    loss_ref[...] = jnp.log(sums_ref[:1, :count]) - sums_ref[1:2, :count]
 
 
 def query_kernel(first, *refs):
@@ -177,11 +199,15 @@
     out_ref[...] = (qdir - wide(q_ref[:, at]) * column_ref[:, :1]).astype(BF16)
 
 
-def far_kernel(kept_ref, got_ref, *out_refs):
-    total = kept_ref[...] + wide(got_ref[...])
-    part = out_refs[0].shape[0]
-    for k, ref in enumerate(out_refs):
-        ref[...] = total[k * part : (k + 1) * part].astype(ref.dtype)
+def far_kernel(n, *refs):
+    at = 0
+    for kept_ref, got_ref in zip(refs[:n], refs[n : 2 * n]):
+        total = kept_ref[...] + wide(got_ref[...])
+        columns = slice(at, at + total.shape[1])
+        at += total.shape[1]
+        part = refs[2 * n].shape[0]
+        for k, ref in enumerate(refs[2 * n :]):
+            ref[:, columns] = total[k * part : (k + 1) * part].astype(ref.dtype)
 
 
 def passage_kernel(n, p_ref, total_ref, *refs):
@@ -245,21 +271,33 @@
             in_specs=[SMEM] + [VMEM] * (n + 8),
             flops=2 * half * count * width,
         )
-        kept, sent, qc, share, loss, inner = call(
+        piece = (half // 2, width // 2)
+        kept0, sent0, coef, sums = call(
             coef_kernel,
-            [((half // 2, width), F32), ((half // 2, width), BF16), ((half, count), BF16), ((half + 8, count), F32)]
-            + [((1, count), F32)] * 2,
-            (queries, others, raw, scale, qs, terms, chosen, sums, cross(sums, core), row(d_loss), pack),
-            flops=4 * half * count * width,
-        )
-
-        got = cross(sent, stages[-2][1])
+            [(piece, F32), (piece, BF16), ((half, both), F32), ((8, both), F32)],
+            (queries, others, qs, terms, chosen, sums, cross(sums, core), row(d_loss), pack),
+            flops=2 * half * count * width,
+        )
+        near = stages[-2][1]
+        got0 = cross(sent0, near)
+        kept1, sent1 = call(
+            other_columns_kernel, [(piece, F32), (piece, BF16)], (queries, others, coef), flops=2 * half * count * width
+        )
+        qc, share, loss, inner = call(
+            share_kernel,
+            [((half, count), BF16), ((half + 8, count), F32)] + [((1, count), F32)] * 2,
+            (raw, scale, coef, sums),
+        )
+
+        kept, got = [kept0, kept1], [got0, cross(sent1, near)]
         for _, m in stages[1:-2][::-1]:
-            total = kept + wide(got)
+            total = jnp.concatenate(kept, axis=1) + wide(jnp.concatenate(got, axis=1))
             part = total.shape[0] // 2
-            kept, got = total[:part], cross(total[part:].astype(BF16), m)
+            kept, got = [total[:part]], [cross(total[part:].astype(BF16), m)]
         term = (block, width)
-        total, *terms = call(far_kernel, [(term, F32)] + [(term, BF16)] * 3, (kept, got))
+        total, *terms = call(
+            functools.partial(far_kernel, len(kept)), [(term, F32)] + [(term, BF16)] * 3, (*kept, *got)
+        )
         moved = [cross(terms[k - 1], stages[0][k]) for k in (3, 2, 1)]
         for t in moved:
             total = total + wide(t)

time: 47.1 us -> 48.5 us (1.030)
  Pallas kernels: 15.7 us -> 17.4 us
  waiting for transfers between devices: 13.9 us -> 13.1 us
    pallas_call x8 -> x10, Pallas kernels: 15.7 us -> 17.4 us  [call(): pl.pallas_call(kernel, out_shape=tuple((jax.ShapeDtypeStruct(*out) for ou...]
    ppermute x15 -> x16, waiting for transfers between devices: 13.9 us -> 13.1 us  [swap(): return lax.ppermute(x, axis, [(i, i ^ mask) for i in range(size)])]
    ppermute x15 -> x16, starting transfers between devices: 15.5 us -> 15.9 us  [swap(): return lax.ppermute(x, axis, [(i, i ^ mask) for i in range(size)])]
  transfers between devices with their start and end apart: 15 -> 16, of which waited for: 7 -> 8; matrix products, arithmetic and copies ran while one was open for 2% -> 2% of each run, Pallas kernels for 11% -> 17%
where the time goes in v2:
time: 48.5 us; the launch traced here: 48.1 us
  Pallas kernels  17.4 us (36%)
  starting transfers between devices  15.9 us (33%)
  waiting for transfers between devices  13.1 us (27%)
  other arithmetic  0.87 us (2%)
  between operations  0.74 us (2%)
    pallas_call x10, Pallas kernels, call(): pl.pallas_call(kernel, out_shape=tuple((jax.ShapeDtypeStruct(*out) for ou...  17.4 us
    ppermute x16, starting transfers between devices, swap(): return lax.ppermute(x, axis, [(i, i ^ mask) for i in range(size)])  15.9 us
    ppermute x16, waiting for transfers between devices, swap(): return lax.ppermute(x, axis, [(i, i ^ mask) for i in range(size)])  13.1 us
  transfers between devices with their start and end apart: 16, of which 8 were waited for; matrix products, arithmetic and copies ran while one was open for 2% of the time, Pallas kernels for 17%

profile of v2, /device:TPU:0, one launch (start us, length us, event | category | flops | bytes accessed | tf_op | source)
XLA Modules:
  0.0 48.1 jit_solution(17855249033335855274)
XLA Ops:
  0.6 0.0 copy-start
  0.6 0.6 %collective-permute-start.5 = (bf16[256,4096]{1,0:T(8,128)(2,1)}, bf16[256,4096]{1,0:T(8,128)(2,1)}, u32[]{:S(2)}, u32[]{:S(2)}) collective-permute-start(bf16[256,4096]{1,0:T(8,128)(2,1)} %q_ref.1), channel_id=1, source_target_pairs={{0,2},{2,0},{4,6},{6,4},{8,10},{10,8},{12,14},{14,12},{16,18},{18,... | collective-permute-start | bytes 6291464 | tf_op jit(solution)/shard_map/ppermute | solution.py:32
  1.2 3.7 %collective-permute-start.1 = (bf16[4,4096]{1,0:T(4,128)(2,1)}, bf16[4,4096]{1,0:T(4,128)(2,1)S(1)}, u32[]{:S(2)}, u32[]{:S(2)}) collective-permute-start(bf16[4,4096]{1,0:T(4,128)(2,1)} %p_ref.1), channel_id=1, source_target_pairs={{0,18},{2,16},{4,22},{6,20},{8,26},{10,24},{12,30},{14,28},{16,2},... | collective-permute-start | bytes 98312 | tf_op jit(solution)/shard_map/ppermute | solution.py:32
  4.9 1.0 %collective-permute-start.2 = (bf16[4,4096]{1,0:T(4,128)(2,1)}, bf16[4,4096]{1,0:T(4,128)(2,1)S(1)}, u32[]{:S(2)}, u32[]{:S(2)}) collective-permute-start(bf16[4,4096]{1,0:T(4,128)(2,1)} %p_ref.1), channel_id=1, source_target_pairs={{0,26},{2,24},{4,30},{6,28},{8,18},{10,16},{12,22},{14,20},{16,10}... | collective-permute-start | bytes 98312 | tf_op jit(solution)/shard_map/ppermute | solution.py:32
  5.9 0.2 collective-permute-start
  6.2 0.6 %collective-permute-done.1 = bf16[4,4096]{1,0:T(4,128)(2,1)S(1)} collective-permute-done((bf16[4,4096]{1,0:T(4,128)(2,1)}, bf16[4,4096]{1,0:T(4,128)(2,1)S(1)}, u32[]{:S(2)}, u32[]{:S(2)}) %collective-permute-start.1) | collective-permute-done | bytes 32800 | tf_op jit(solution)/shard_map/ppermute | solution.py:32
  6.8 3.6 %collective-permute-done.2 = bf16[4,4096]{1,0:T(4,128)(2,1)S(1)} collective-permute-done((bf16[4,4096]{1,0:T(4,128)(2,1)}, bf16[4,4096]{1,0:T(4,128)(2,1)S(1)}, u32[]{:S(2)}, u32[]{:S(2)}) %collective-permute-start.2) | collective-permute-done | bytes 32800 | tf_op jit(solution)/shard_map/ppermute | solution.py:32
  10.5 1.4 %collective-permute-start.4 = (bf16[8,4096]{1,0:T(8,128)(2,1)S(1)}, bf16[8,4096]{1,0:T(8,128)(2,1)S(1)}, u32[]{:S(2)}, u32[]{:S(2)}) collective-permute-start(bf16[8,4096]{1,0:T(8,128)(2,1)S(1)} %pad_maximum_fusion.1.refs_1_), channel_id=1, source_target_pairs={{0,6},{2,4},{4,2},{6,0},{8,14},{10,12},{12,10},{14,8},{16,22},{18,... | collective-permute-start | bytes 196616 | tf_op jit(solution)/shard_map/ppermute | solution.py:32
  11.9 0.0 collective-permute-done
  11.9 0.8 %pad_maximum_fusion.refs_0_ = bf16[8,4096]{1,0:T(8,128)(2,1)S(1)} fusion(bf16[4,4096]{1,0:T(4,128)(2,1)S(1)} %collective-permute-done, bf16[4,4096]{1,0:T(4,128)(2,1)} %p_ref.1), kind=kLoop, calls=%fused_computation | loop fusion | flops 131072 | bytes 131072 | tf_op jit(solution)/shard_map/concatenate | solution.py:239
  12.7 0.4 collective-permute-start.3
  13.1 1.7 %shard_map.95 = (f32[32,256]{1,0:T(8,128)}, f32[40,256]{1,0:T(8,128)}) custom-call(s32[1]{0:T(128)} %bitcast.me_ref, s32[32,256]{1,0:T(8,128)} %bitcast.11, s32[32,256]{1,0:T(8,128)} %bitcast.12, s32[1,256]{1,0:T(1,128)} %bitcast.13, s32[1,256]{1,0:T(1,128)} %bitcast.7, f32[1,256]{1,0:T(1,128)} %bitcast.9, bf16[256,4096]{1,0:T(8,128)(2,1)} %q_ref.1), custom_call_target="tpu_custom_call" | custom-call | flops 10000000 | bytes 1000000 | tf_op jit(solution)/shard_map/pallas_call | solution.py:41
  14.8 0.0 copy-start.2
  14.8 0.0 copy-start.3
  14.8 0.3 collective-permute-start.6
  15.2 0.0 collective-permute-done.5.refs_3_.refs_5_.refs_1_.other_ref
  15.2 0.0 copy-done
  15.2 2.8 %shard_map.94 = (f32[16,512]{1,0:T(8,128)S(1)}, f32[16,128]{1,0:T(8,128)S(1)}, f32[1,512]{1,0:T(1,128)S(1)}) custom-call(bf16[8,4096]{1,0:T(8,128)(2,1)S(1)} %pad_maximum_fusion.refs_0_, bf16[8,4096]{1,0:T(8,128)(2,1)S(1)} %pad_maximum_fusion.1.refs_1_, bf16[256,4096]{1,0:T(8,128)(2,1)S(1)} %copy-done, ...), custom_call_target="tpu_custom_call" | custom-call | flops 67108864 | bytes 1000000 | tf_op jit(solution)/shard_map/pallas_call | solution.py:41
  17.9 0.0 collective-permute-done.6.refs_10_.refs_8_
  17.9 0.0 collective-permute-done.4.refs_3_
  18.0 0.0 collective-permute-done.3.refs_2_
  18.0 0.0 copy-start.4
  18.0 2.8 %shard_map.96 = (bf16[32,4096]{1,0:T(8,128)(2,1)S(1)}, f32[32,512]{1,0:T(8,128)S(1)}, f32[32,128]{1,0:T(8,128)S(1)}, f32[32,512]{1,0:T(8,128)S(1)}, f32[32,512]{1,0:T(8,128)S(1)}, /*index=5*/f32[8,512]{1,0:T(8,128)S(1)}) custom-call(s32[1]{0:T(128)} %bitcast.me_ref, bf16[8,4096]{1,0:T(8,128)(2,1)S(1)} %pad_maximum_fusion.refs_0_, ...), custom_call_target="tpu_custom_call" | custom-call | flops 67108864 | bytes 1000000 | tf_op jit(solution)/shard_map/pallas_call | solution.py:41
  20.8 0.3 collective-permute-start.7
  21.2 0.9 %collective-permute-done.7.refs_6_ = f32[8,512]{1,0:T(8,128)S(1)} collective-permute-done((f32[8,512]{1,0:T(8,128)S(1)}, f32[8,512]{1,0:T(8,128)S(1)}, u32[]{:S(2)}, u32[]{:S(2)}) %collective-permute-start.7) | collective-permute-done | bytes 16416 | tf_op jit(solution)/shard_map/ppermute | solution.py:32
  22.1 2.1 %shard_map.97 = (f32[16,2048]{1,0:T(8,128)S(1)}, bf16[16,2048]{1,0:T(8,128)(2,1)S(1)}, f32[32,512]{1,0:T(8,128)S(1)}, f32[8,512]{1,0:T(8,128)S(1)}) custom-call(bf16[256,4096]{1,0:T(8,128)(2,1)S(1)} %copy-done, bf16[256,4096]{1,0:T(8,128)(2,1)} %collective-permute-done.5.refs_3_.refs_5_.refs_1_.other_ref, ...), custom_call_target="tpu_custom_call" | custom-call | flops 67108864 | bytes 1000000 | tf_op jit(solution)/shard_map/pallas_call | solution.py:41
  24.2 1.4 %collective-permute-start.10 = (bf16[16,2048]{1,0:T(8,128)(2,1)S(1)}, bf16[16,2048]{1,0:T(8,128)(2,1)S(1)}, u32[]{:S(2)}, u32[]{:S(2)}) collective-permute-start(bf16[16,2048]{1,0:T(8,128)(2,1)S(1)} %get-tuple-element.47), channel_id=1, source_target_pairs={{0,6},{2,4},{4,2},{6,0},{8,14},{10,12},{12,10},{14,8},{16,22},{18,... | collective-permute-start | bytes 196616 | tf_op jit(solution)/shard_map/ppermute | solution.py:32
  25.6 2.1 %shard_map.101 = (f32[16,2048]{1,0:T(8,128)S(1)}, bf16[16,2048]{1,0:T(8,128)(2,1)S(1)}) custom-call(bf16[256,4096]{1,0:T(8,128)(2,1)S(1)} %copy-done, bf16[256,4096]{1,0:T(8,128)(2,1)} %collective-permute-done.5.refs_3_.refs_5_.refs_1_.other_ref, f32[32,512]{1,0:T(8,128)S(1)} %get-tuple-element.38.coef_ref), custom_call_target="tpu_custom_call" | custom-call | flops 67108864 | bytes 1000000 | tf_op jit(solution)/shard_map/pallas_call | solution.py:41
  27.7 0.4 collective-permute-start.11
  28.0 0.1 collective-permute-done.10.refs_2_
  28.1 3.5 %collective-permute-done.11.refs_3_ = bf16[16,2048]{1,0:T(8,128)(2,1)S(1)} collective-permute-done((bf16[16,2048]{1,0:T(8,128)(2,1)S(1)}, bf16[16,2048]{1,0:T(8,128)(2,1)S(1)}, u32[]{:S(2)}, u32[]{:S(2)}) %collective-permute-start.11) | collective-permute-done | bytes 65568 | tf_op jit(solution)/shard_map/ppermute | solution.py:32
  31.7 1.2 %collective-permute-start.12 = (bf16[4,4096]{1,0:T(4,128)(2,1)S(1)}, bf16[4,4096]{1,0:T(4,128)(2,1)S(1)}, u32[]{:S(2)}, u32[]{:S(2)}) collective-permute-start(bf16[4,4096]{1,0:T(4,128)(2,1)S(1)} %get-tuple-element.50), channel_id=1, source_target_pairs={{0,26},{2,24},{4,30},{6,28},{8,18},{10,16},{12,22},{14,20},{16,10}... | collective-permute-start | bytes 98312 | tf_op jit(solution)/shard_map/ppermute | solution.py:32
  32.9 0.0 collective-permute-start.13
  32.9 2.8 %collective-permute-start.14 = (bf16[4,4096]{1,0:T(4,128)(2,1)S(1)}, bf16[4,4096]{1,0:T(4,128)(2,1)S(1)}, u32[]{:S(2)}, u32[]{:S(2)}) collective-permute-start(bf16[4,4096]{1,0:T(4,128)(2,1)S(1)} %get-tuple-element.52), channel_id=1, source_target_pairs={{0,10},{2,8},{4,14},{6,12},{8,2},{10,0},{12,6},{14,4},{16,26},{18,... | collective-permute-start | bytes 98312 | tf_op jit(solution)/shard_map/ppermute | solution.py:32
  35.7 0.3 collective-permute-start.8
  36.0 0.6 %shard_map.98 = (bf16[32,256]{1,0:T(8,128)(2,1)S(1)}, f32[40,256]{1,0:T(8,128)S(1)}, f32[1,256]{1,0:T(1,128)}, f32[1,256]{1,0:T(1,128)S(1)}) custom-call(f32[32,512]{1,0:T(8,128)S(1)} %get-tuple-element.33.raw_ref, f32[32,128]{1,0:T(8,128)S(1)} %get-tuple-element.34.scale_ref, f32[32,512]{1,0:T(8,128)S(1)} %get-tuple-element.38.coef_ref, ...), custom_call_target="tpu_custom_call" | custom-call | flops 200000 | bytes 1000000 | tf_op jit(solution)/shard_map/pallas_call | solution.py:41
  36.6 0.2 collective-permute-start.9
  36.8 0.1 collective-permute-done.12
  36.9 1.7 %collective-permute-done.13 = bf16[4,4096]{1,0:T(4,128)(2,1)S(1)} collective-permute-done((bf16[4,4096]{1,0:T(4,128)(2,1)S(1)}, bf16[4,4096]{1,0:T(4,128)(2,1)S(1)}, u32[]{:S(2)}, u32[]{:S(2)}) %collective-permute-start.13) | collective-permute-done | bytes 32800 | tf_op jit(solution)/shard_map/ppermute | solution.py:32
  38.6 0.0 collective-permute-done.14
  38.7 1.6 %collective-permute-start.15 = (bf16[4,4096]{1,0:T(4,128)(2,1)S(1)}, bf16[4,4096]{1,0:T(4,128)(2,1)S(1)}, u32[]{:S(2)}, u32[]{:S(2)}) collective-permute-start(bf16[4,4096]{1,0:T(4,128)(2,1)S(1)} %get-tuple-element.53), channel_id=1, source_target_pairs={{0,1},{1,0},{2,3},{3,2},{4,5},{5,4},{6,7},{7,6},{8,9},{9,8},{10,11... | collective-permute-start | bytes 98312 | tf_op jit(solution)/shard_map/ppermute | solution.py:32
  40.2 2.4 %collective-permute-done.15.refs_0_ = bf16[4,4096]{1,0:T(4,128)(2,1)S(1)} collective-permute-done((bf16[4,4096]{1,0:T(4,128)(2,1)S(1)}, bf16[4,4096]{1,0:T(4,128)(2,1)S(1)}, u32[]{:S(2)}, u32[]{:S(2)}) %collective-permute-start.15) | collective-permute-done | bytes 32800 | tf_op jit(solution)/shard_map/ppermute | solution.py:32
  42.7 0.0 copy-done.1
  42.7 0.9 %shard_map.103 = bf16[4,4096]{1,0:T(4,128)(2,1)} custom-call(bf16[4,4096]{1,0:T(4,128)(2,1)S(1)} %copy-done.1, f32[4,4096]{1,0:T(4,128)S(1)} %get-tuple-element.54.total_ref, bf16[4,4096]{1,0:T(4,128)(2,1)S(1)} %collective-permute-done.15.refs_0_), custom_call_target="tpu_custom_call" | custom-call | flops 200000 | bytes 1000000 | tf_op jit(solution)/shard_map/pallas_call | solution.py:41
  43.5 0.0 collective-permute-done.9.refs_3_
  43.5 0.0 collective-permute-done.8.refs_1_
  43.5 2.3 %shard_map.99.refs_7_ = bf16[256,4096]{1,0:T(8,128)(2,1)} custom-call(bf16[32,4096]{1,0:T(8,128)(2,1)S(1)} %get-tuple-element.41.refs_0_, bf16[32,4096]{1,0:T(8,128)(2,1)S(1)} %collective-permute-done.8.refs_1_, bf16[32,256]{1,0:T(8,128)(2,1)S(1)} %get-tuple-element.42.refs_2_, f32[40,256]{1,0:T(8,128)S(1)} %collective-permute-done.9.refs_3_, ...), custom_call_target="tpu_custom_call" | custom-call | flops 67108864 | bytes 3000000 | tf_op jit(solution)/shard_map/pallas_call | solution.py:41
  45.8 2.3 %shard_map.100 = bf16[256,4096]{1,0:T(8,128)(2,1)} custom-call(bf16[32,4096]{1,0:T(8,128)(2,1)S(1)} %get-tuple-element.41.refs_0_, bf16[32,4096]{1,0:T(8,128)(2,1)S(1)} %collective-permute-done.8.refs_1_, bf16[32,256]{1,0:T(8,128)(2,1)S(1)} %get-tuple-element.42.refs_2_, ...), custom_call_target="tpu_custom_call", output_to_operand_aliasing={{}: (7, {})} | custom-call | flops 67108864 | bytes 3000000 | tf_op jit(solution)/shard_map/pallas_call | solution.py:41
  (7 shorter events, 0.1 us)
Async XLA Ops:
  0.6 14.5 %copy-start = (bf16[256,4096]{1,0:T(8,128)(2,1)S(1)}, bf16[256,4096]{1,0:T(8,128)(2,1)}, u32[]{:S(2)}) copy-start(bf16[256,4096]{1,0:T(8,128)(2,1)} %q_ref.1) | copy-start | bytes 6291460
  0.6 14.5 %collective-permute-start.5 = (bf16[256,4096]{1,0:T(8,128)(2,1)}, bf16[256,4096]{1,0:T(8,128)(2,1)}, u32[]{:S(2)}, u32[]{:S(2)}) collective-permute-start(bf16[256,4096]{1,0:T(8,128)(2,1)} %q_ref.1), channel_id=1, source_target_pairs={{0,2},{2,0},{4,6},{6,4},{8,10},{10,8},{12,14},{14,12},{16,18},{18,... | collective-permute-start | bytes 6291464 | tf_op jit(solution)/shard_map/ppermute | solution.py:32
  1.2 5.6 %collective-permute-start.1 = (bf16[4,4096]{1,0:T(4,128)(2,1)}, bf16[4,4096]{1,0:T(4,128)(2,1)S(1)}, u32[]{:S(2)}, u32[]{:S(2)}) collective-permute-start(bf16[4,4096]{1,0:T(4,128)(2,1)} %p_ref.1), channel_id=1, source_target_pairs={{0,18},{2,16},{4,22},{6,20},{8,26},{10,24},{12,30},{14,28},{16,2},... | collective-permute-start | bytes 98312 | tf_op jit(solution)/shard_map/ppermute | solution.py:32
  4.9 5.5 %collective-permute-start.2 = (bf16[4,4096]{1,0:T(4,128)(2,1)}, bf16[4,4096]{1,0:T(4,128)(2,1)S(1)}, u32[]{:S(2)}, u32[]{:S(2)}) collective-permute-start(bf16[4,4096]{1,0:T(4,128)(2,1)} %p_ref.1), channel_id=1, source_target_pairs={{0,26},{2,24},{4,30},{6,28},{8,18},{10,16},{12,22},{14,20},{16,10}... | collective-permute-start | bytes 98312 | tf_op jit(solution)/shard_map/ppermute | solution.py:32
  5.9 6.0 %collective-permute-start = (bf16[4,4096]{1,0:T(4,128)(2,1)}, bf16[4,4096]{1,0:T(4,128)(2,1)S(1)}, u32[]{:S(2)}, u32[]{:S(2)}) collective-permute-start(bf16[4,4096]{1,0:T(4,128)(2,1)} %p_ref.1), channel_id=1, source_target_pairs={{0,10},{2,8},{4,14},{6,12},{8,2},{10,0},{12,6},{14,4},{16,26},{18,... | collective-permute-start | bytes 98312 | tf_op jit(solution)/shard_map/ppermute | solution.py:32
  10.5 7.5 %collective-permute-start.4 = (bf16[8,4096]{1,0:T(8,128)(2,1)S(1)}, bf16[8,4096]{1,0:T(8,128)(2,1)S(1)}, u32[]{:S(2)}, u32[]{:S(2)}) collective-permute-start(bf16[8,4096]{1,0:T(8,128)(2,1)S(1)} %pad_maximum_fusion.1.refs_1_), channel_id=1, source_target_pairs={{0,6},{2,4},{4,2},{6,0},{8,14},{10,12},{12,10},{14,8},{16,22},{18,... | collective-permute-start | bytes 196616 | tf_op jit(solution)/shard_map/ppermute | solution.py:32
  12.7 5.3 %collective-permute-start.3 = (bf16[8,4096]{1,0:T(8,128)(2,1)S(1)}, bf16[8,4096]{1,0:T(8,128)(2,1)S(1)}, u32[]{:S(2)}, u32[]{:S(2)}) collective-permute-start(bf16[8,4096]{1,0:T(8,128)(2,1)S(1)} %pad_maximum_fusion.refs_0_), channel_id=1, source_target_pairs={{0,6},{2,4},{4,2},{6,0},{8,14},{10,12},{12,10},{14,8},{16,22},{18,... | collective-permute-start | bytes 196616 | tf_op jit(solution)/shard_map/ppermute | solution.py:32
  14.8 3.2 %copy-start.2 = (f32[32,256]{1,0:T(8,128)S(1)}, f32[32,256]{1,0:T(8,128)}, u32[]{:S(2)}) copy-start(f32[32,256]{1,0:T(8,128)} %get-tuple-element.31.refs_9_) | copy-start | bytes 98308
  14.8 3.1 %copy-start.3 = (s32[256]{0:T(256)S(1)}, s32[256]{0:T(256)}, u32[]{:S(2)}) copy-start(s32[256]{0:T(256)} %param.9) | copy-start | bytes 3076
  14.8 3.1 %collective-permute-start.6 = (f32[40,256]{1,0:T(8,128)}, f32[40,256]{1,0:T(8,128)S(1)}, u32[]{:S(2)}, u32[]{:S(2)}) collective-permute-start(f32[40,256]{1,0:T(8,128)} %get-tuple-element.32), channel_id=1, source_target_pairs={{0,2},{2,0},{4,6},{6,4},{8,10},{10,8},{12,14},{14,12},{16,18},{18,... | collective-permute-start | bytes 122888 | tf_op jit(solution)/shard_map/ppermute | solution.py:32
  18.0 4.1 %copy-start.4 = (f32[256]{0:T(256)S(1)}, f32[256]{0:T(256)}, u32[]{:S(2)}) copy-start(f32[256]{0:T(256)} %param.13) | copy-start | bytes 3076
  20.8 1.2 %collective-permute-start.7 = (f32[8,512]{1,0:T(8,128)S(1)}, f32[8,512]{1,0:T(8,128)S(1)}, u32[]{:S(2)}, u32[]{:S(2)}) collective-permute-start(f32[8,512]{1,0:T(8,128)S(1)} %get-tuple-element.37.refs_5_), channel_id=1, source_target_pairs={{0,2},{2,0},{4,6},{6,4},{8,10},{10,8},{12,14},{14,12},{16,18},{18,... | collective-permute-start | bytes 49160 | tf_op jit(solution)/shard_map/ppermute | solution.py:32
  24.2 4.0 %collective-permute-start.10 = (bf16[16,2048]{1,0:T(8,128)(2,1)S(1)}, bf16[16,2048]{1,0:T(8,128)(2,1)S(1)}, u32[]{:S(2)}, u32[]{:S(2)}) collective-permute-start(bf16[16,2048]{1,0:T(8,128)(2,1)S(1)} %get-tuple-element.47), channel_id=1, source_target_pairs={{0,6},{2,4},{4,2},{6,0},{8,14},{10,12},{12,10},{14,8},{16,22},{18,... | collective-permute-start | bytes 196616 | tf_op jit(solution)/shard_map/ppermute | solution.py:32
  25.6 17.1 %copy-start.1 = (bf16[4,4096]{1,0:T(4,128)(2,1)S(1)}, bf16[4,4096]{1,0:T(4,128)(2,1)}, u32[]{:S(2)}) copy-start(bf16[4,4096]{1,0:T(4,128)(2,1)} %p_ref.1) | copy-start | bytes 98308
  27.7 4.0 %collective-permute-start.11 = (bf16[16,2048]{1,0:T(8,128)(2,1)S(1)}, bf16[16,2048]{1,0:T(8,128)(2,1)S(1)}, u32[]{:S(2)}, u32[]{:S(2)}) collective-permute-start(bf16[16,2048]{1,0:T(8,128)(2,1)S(1)} %get-tuple-element.48), channel_id=1, source_target_pairs={{0,6},{2,4},{4,2},{6,0},{8,14},{10,12},{12,10},{14,8},{16,22},{18,... | collective-permute-start | bytes 196616 | tf_op jit(solution)/shard_map/ppermute | solution.py:32
  31.7 5.2 %collective-permute-start.12 = (bf16[4,4096]{1,0:T(4,128)(2,1)S(1)}, bf16[4,4096]{1,0:T(4,128)(2,1)S(1)}, u32[]{:S(2)}, u32[]{:S(2)}) collective-permute-start(bf16[4,4096]{1,0:T(4,128)(2,1)S(1)} %get-tuple-element.50), channel_id=1, source_target_pairs={{0,26},{2,24},{4,30},{6,28},{8,18},{10,16},{12,22},{14,20},{16,10}... | collective-permute-start | bytes 98312 | tf_op jit(solution)/shard_map/ppermute | solution.py:32
  32.9 5.8 %collective-permute-start.13 = (bf16[4,4096]{1,0:T(4,128)(2,1)S(1)}, bf16[4,4096]{1,0:T(4,128)(2,1)S(1)}, u32[]{:S(2)}, u32[]{:S(2)}) collective-permute-start(bf16[4,4096]{1,0:T(4,128)(2,1)S(1)} %get-tuple-element.51), channel_id=1, source_target_pairs={{0,18},{2,16},{4,22},{6,20},{8,26},{10,24},{12,30},{14,28},{16,2},... | collective-permute-start | bytes 98312 | tf_op jit(solution)/shard_map/ppermute | solution.py:32
  32.9 5.8 %collective-permute-start.14 = (bf16[4,4096]{1,0:T(4,128)(2,1)S(1)}, bf16[4,4096]{1,0:T(4,128)(2,1)S(1)}, u32[]{:S(2)}, u32[]{:S(2)}) collective-permute-start(bf16[4,4096]{1,0:T(4,128)(2,1)S(1)} %get-tuple-element.52), channel_id=1, source_target_pairs={{0,10},{2,8},{4,14},{6,12},{8,2},{10,0},{12,6},{14,4},{16,26},{18,... | collective-permute-start | bytes 98312 | tf_op jit(solution)/shard_map/ppermute | solution.py:32
  35.7 7.8 %collective-permute-start.8 = (bf16[32,4096]{1,0:T(8,128)(2,1)S(1)}, bf16[32,4096]{1,0:T(8,128)(2,1)S(1)}, u32[]{:S(2)}, u32[]{:S(2)}) collective-permute-start(bf16[32,4096]{1,0:T(8,128)(2,1)S(1)} %get-tuple-element.41.refs_0_), channel_id=1, source_target_pairs={{0,2},{2,0},{4,6},{6,4},{8,10},{10,8},{12,14},{14,12},{16,18},{18,... | collective-permute-start | bytes 786440 | tf_op jit(solution)/shard_map/ppermute | solution.py:32
  36.6 7.0 %collective-permute-start.9 = (f32[40,256]{1,0:T(8,128)S(1)}, f32[40,256]{1,0:T(8,128)S(1)}, u32[]{:S(2)}, u32[]{:S(2)}) collective-permute-start(f32[40,256]{1,0:T(8,128)S(1)} %get-tuple-element.43), channel_id=1, source_target_pairs={{0,2},{2,0},{4,6},{6,4},{8,10},{10,8},{12,14},{14,12},{16,18},{18,... | collective-permute-start | bytes 122888 | tf_op jit(solution)/shard_map/ppermute | solution.py:32
  38.7 4.0 %collective-permute-start.15 = (bf16[4,4096]{1,0:T(4,128)(2,1)S(1)}, bf16[4,4096]{1,0:T(4,128)(2,1)S(1)}, u32[]{:S(2)}, u32[]{:S(2)}) collective-permute-start(bf16[4,4096]{1,0:T(4,128)(2,1)S(1)} %get-tuple-element.53), channel_id=1, source_target_pairs={{0,1},{1,0},{2,3},{3,2},{4,5},{5,4},{6,7},{7,6},{8,9},{9,8},{10,11... | collective-permute-start | bytes 98312 | tf_op jit(solution)/shard_map/ppermute | solution.py:32

commit v3 on v2

--- a/solution.py
+++ b/solution.py
@@ -271,7 +271,8 @@
             in_specs=[SMEM] + [VMEM] * (n + 8),
             flops=2 * half * count * width,
         )
-        piece = (half // 2, width // 2)
+        lead = width // 16 * 11
+        piece = (half // 2, lead)
         kept0, sent0, coef, sums = call(
             coef_kernel,
             [(piece, F32), (piece, BF16), ((half, both), F32), ((8, both), F32)],
@@ -281,7 +282,10 @@
         near = stages[-2][1]
         got0 = cross(sent0, near)
         kept1, sent1 = call(
-            other_columns_kernel, [(piece, F32), (piece, BF16)], (queries, others, coef), flops=2 * half * count * width
+            other_columns_kernel,
+            [((half // 2, width - lead), F32), ((half // 2, width - lead), BF16)],
+            (queries, others, coef),
+            flops=2 * half * count * width,
         )
         qc, share, loss, inner = call(
             share_kernel,

time: 48.5 us -> 48 us (0.990)
  waiting for transfers between devices: 13.1 us -> 12.6 us
    ppermute x16, waiting for transfers between devices: 13.1 us -> 12.6 us  [swap(): return lax.ppermute(x, axis, [(i, i ^ mask) for i in range(size)])]
  transfers between devices with their start and end apart: 16 -> 16, of which waited for: 8 -> 7; matrix products, arithmetic and copies ran while one was open for 2% -> 2% of each run, Pallas kernels for 17% -> 16%
where the time goes in v3:
time: 48 us; the launch traced here: 47.6 us
  Pallas kernels  17.5 us (36%)
  starting transfers between devices  15.9 us (33%)
  waiting for transfers between devices  12.6 us (26%)
  other arithmetic  0.87 us (2%)
  between operations  0.74 us (2%)
    pallas_call x10, Pallas kernels, call(): pl.pallas_call(kernel, out_shape=tuple((jax.ShapeDtypeStruct(*out) for ou...  17.5 us
    ppermute x16, starting transfers between devices, swap(): return lax.ppermute(x, axis, [(i, i ^ mask) for i in range(size)])  15.9 us
    ppermute x16, waiting for transfers between devices, swap(): return lax.ppermute(x, axis, [(i, i ^ mask) for i in range(size)])  12.6 us
  transfers between devices with their start and end apart: 16, of which 7 were waited for; matrix products, arithmetic and copies ran while one was open for 2% of the time, Pallas kernels for 16%

profile of v3, /device:TPU:0, one launch (start us, length us, event | category | flops | bytes accessed | tf_op | source)
XLA Modules:
  0.0 47.6 jit_solution(11487269828414450088)
XLA Ops:
  0.6 0.0 copy-start
  0.6 0.6 %collective-permute-start.5 = (bf16[256,4096]{1,0:T(8,128)(2,1)}, bf16[256,4096]{1,0:T(8,128)(2,1)}, u32[]{:S(2)}, u32[]{:S(2)}) collective-permute-start(bf16[256,4096]{1,0:T(8,128)(2,1)} %q_ref.1), channel_id=1, source_target_pairs={{0,2},{2,0},{4,6},{6,4},{8,10},{10,8},{12,14},{14,12},{16,18},{18,... | collective-permute-start | bytes 6291464 | tf_op jit(solution)/shard_map/ppermute | solution.py:32
  1.2 3.7 %collective-permute-start.1 = (bf16[4,4096]{1,0:T(4,128)(2,1)}, bf16[4,4096]{1,0:T(4,128)(2,1)S(1)}, u32[]{:S(2)}, u32[]{:S(2)}) collective-permute-start(bf16[4,4096]{1,0:T(4,128)(2,1)} %p_ref.1), channel_id=1, source_target_pairs={{0,18},{2,16},{4,22},{6,20},{8,26},{10,24},{12,30},{14,28},{16,2},... | collective-permute-start | bytes 98312 | tf_op jit(solution)/shard_map/ppermute | solution.py:32
  4.9 1.0 %collective-permute-start.2 = (bf16[4,4096]{1,0:T(4,128)(2,1)}, bf16[4,4096]{1,0:T(4,128)(2,1)S(1)}, u32[]{:S(2)}, u32[]{:S(2)}) collective-permute-start(bf16[4,4096]{1,0:T(4,128)(2,1)} %p_ref.1), channel_id=1, source_target_pairs={{0,26},{2,24},{4,30},{6,28},{8,18},{10,16},{12,22},{14,20},{16,10}... | collective-permute-start | bytes 98312 | tf_op jit(solution)/shard_map/ppermute | solution.py:32
  5.9 0.2 collective-permute-start
  6.2 0.6 %collective-permute-done.1 = bf16[4,4096]{1,0:T(4,128)(2,1)S(1)} collective-permute-done((bf16[4,4096]{1,0:T(4,128)(2,1)}, bf16[4,4096]{1,0:T(4,128)(2,1)S(1)}, u32[]{:S(2)}, u32[]{:S(2)}) %collective-permute-start.1) | collective-permute-done | bytes 32800 | tf_op jit(solution)/shard_map/ppermute | solution.py:32
  6.8 3.6 %collective-permute-done.2 = bf16[4,4096]{1,0:T(4,128)(2,1)S(1)} collective-permute-done((bf16[4,4096]{1,0:T(4,128)(2,1)}, bf16[4,4096]{1,0:T(4,128)(2,1)S(1)}, u32[]{:S(2)}, u32[]{:S(2)}) %collective-permute-start.2) | collective-permute-done | bytes 32800 | tf_op jit(solution)/shard_map/ppermute | solution.py:32
  10.5 1.4 %collective-permute-start.4 = (bf16[8,4096]{1,0:T(8,128)(2,1)S(1)}, bf16[8,4096]{1,0:T(8,128)(2,1)S(1)}, u32[]{:S(2)}, u32[]{:S(2)}) collective-permute-start(bf16[8,4096]{1,0:T(8,128)(2,1)S(1)} %pad_maximum_fusion.1.refs_1_), channel_id=1, source_target_pairs={{0,6},{2,4},{4,2},{6,0},{8,14},{10,12},{12,10},{14,8},{16,22},{18,... | collective-permute-start | bytes 196616 | tf_op jit(solution)/shard_map/ppermute | solution.py:32
  11.9 0.0 collective-permute-done
  11.9 0.8 %pad_maximum_fusion.refs_0_ = bf16[8,4096]{1,0:T(8,128)(2,1)S(1)} fusion(bf16[4,4096]{1,0:T(4,128)(2,1)S(1)} %collective-permute-done, bf16[4,4096]{1,0:T(4,128)(2,1)} %p_ref.1), kind=kLoop, calls=%fused_computation | loop fusion | flops 131072 | bytes 131072 | tf_op jit(solution)/shard_map/concatenate | solution.py:239
  12.7 0.4 collective-permute-start.3
  13.1 1.7 %shard_map.95 = (f32[32,256]{1,0:T(8,128)}, f32[40,256]{1,0:T(8,128)}) custom-call(s32[1]{0:T(128)} %bitcast.me_ref, s32[32,256]{1,0:T(8,128)} %bitcast.11, s32[32,256]{1,0:T(8,128)} %bitcast.12, s32[1,256]{1,0:T(1,128)} %bitcast.13, s32[1,256]{1,0:T(1,128)} %bitcast.7, f32[1,256]{1,0:T(1,128)} %bitcast.9, bf16[256,4096]{1,0:T(8,128)(2,1)} %q_ref.1), custom_call_target="tpu_custom_call" | custom-call | flops 10000000 | bytes 1000000 | tf_op jit(solution)/shard_map/pallas_call | solution.py:41
  14.8 0.0 copy-start.2
  14.8 0.0 copy-start.3
  14.8 0.3 collective-permute-start.6
  15.2 0.0 collective-permute-done.5.refs_3_.refs_5_.refs_1_.other_ref
  15.2 0.0 copy-done
  15.2 2.8 %shard_map.94 = (f32[16,512]{1,0:T(8,128)S(1)}, f32[16,128]{1,0:T(8,128)S(1)}, f32[1,512]{1,0:T(1,128)S(1)}) custom-call(bf16[8,4096]{1,0:T(8,128)(2,1)S(1)} %pad_maximum_fusion.refs_0_, bf16[8,4096]{1,0:T(8,128)(2,1)S(1)} %pad_maximum_fusion.1.refs_1_, bf16[256,4096]{1,0:T(8,128)(2,1)S(1)} %copy-done, ...), custom_call_target="tpu_custom_call" | custom-call | flops 67108864 | bytes 1000000 | tf_op jit(solution)/shard_map/pallas_call | solution.py:41
  17.9 0.0 collective-permute-done.6.refs_10_.refs_8_
  17.9 0.0 collective-permute-done.4.refs_3_
  18.0 0.0 collective-permute-done.3.refs_2_
  18.0 0.0 copy-done.2
  18.0 0.0 copy-start.4
  18.0 2.8 %shard_map.96 = (bf16[32,4096]{1,0:T(8,128)(2,1)S(1)}, f32[32,512]{1,0:T(8,128)S(1)}, f32[32,128]{1,0:T(8,128)S(1)}, f32[32,512]{1,0:T(8,128)S(1)}, f32[32,512]{1,0:T(8,128)S(1)}, /*index=5*/f32[8,512]{1,0:T(8,128)S(1)}) custom-call(s32[1]{0:T(128)} %bitcast.me_ref, bf16[8,4096]{1,0:T(8,128)(2,1)S(1)} %pad_maximum_fusion.refs_0_, ...), custom_call_target="tpu_custom_call" | custom-call | flops 67108864 | bytes 1000000 | tf_op jit(solution)/shard_map/pallas_call | solution.py:41
  20.8 0.3 collective-permute-start.7
  21.2 0.9 %collective-permute-done.7.refs_6_ = f32[8,512]{1,0:T(8,128)S(1)} collective-permute-done((f32[8,512]{1,0:T(8,128)S(1)}, f32[8,512]{1,0:T(8,128)S(1)}, u32[]{:S(2)}, u32[]{:S(2)}) %collective-permute-start.7) | collective-permute-done | bytes 16416 | tf_op jit(solution)/shard_map/ppermute | solution.py:32
  22.1 2.2 %shard_map.97 = (f32[16,2816]{1,0:T(8,128)S(1)}, bf16[16,2816]{1,0:T(8,128)(2,1)S(1)}, f32[32,512]{1,0:T(8,128)S(1)}, f32[8,512]{1,0:T(8,128)S(1)}) custom-call(bf16[256,4096]{1,0:T(8,128)(2,1)S(1)} %copy-done, bf16[256,4096]{1,0:T(8,128)(2,1)} %collective-permute-done.5.refs_3_.refs_5_.refs_1_.other_ref, ...), custom_call_target="tpu_custom_call" | custom-call | flops 67108864 | bytes 1000000 | tf_op jit(solution)/shard_map/pallas_call | solution.py:41
  24.3 1.4 %collective-permute-start.10 = (bf16[16,2816]{1,0:T(8,128)(2,1)S(1)}, bf16[16,2816]{1,0:T(8,128)(2,1)S(1)}, u32[]{:S(2)}, u32[]{:S(2)}) collective-permute-start(bf16[16,2816]{1,0:T(8,128)(2,1)S(1)} %get-tuple-element.47), channel_id=1, source_target_pairs={{0,6},{2,4},{4,2},{6,0},{8,14},{10,12},{12,10},{14,8},{16,22},{18,... | collective-permute-start | bytes 270344 | tf_op jit(solution)/shard_map/ppermute | solution.py:32
  25.7 1.9 %shard_map.101 = (f32[16,1280]{1,0:T(8,128)S(1)}, bf16[16,1280]{1,0:T(8,128)(2,1)S(1)}) custom-call(bf16[256,4096]{1,0:T(8,128)(2,1)S(1)} %copy-done, bf16[256,4096]{1,0:T(8,128)(2,1)} %collective-permute-done.5.refs_3_.refs_5_.refs_1_.other_ref, f32[32,512]{1,0:T(8,128)S(1)} %get-tuple-element.38.coef_ref), custom_call_target="tpu_custom_call" | custom-call | flops 67108864 | bytes 1000000 | tf_op jit(solution)/shard_map/pallas_call | solution.py:41
  27.7 0.4 collective-permute-start.11
  28.1 3.1 %collective-permute-done.11.refs_3_ = bf16[16,1280]{1,0:T(8,128)(2,1)S(1)} collective-permute-done((bf16[16,1280]{1,0:T(8,128)(2,1)S(1)}, bf16[16,1280]{1,0:T(8,128)(2,1)S(1)}, u32[]{:S(2)}, u32[]{:S(2)}) %collective-permute-start.11) | collective-permute-done | bytes 40992 | tf_op jit(solution)/shard_map/ppermute | solution.py:32
  31.1 0.0 collective-permute-done.10.refs_2_
  31.2 1.3 %collective-permute-start.12 = (bf16[4,4096]{1,0:T(4,128)(2,1)S(1)}, bf16[4,4096]{1,0:T(4,128)(2,1)S(1)}, u32[]{:S(2)}, u32[]{:S(2)}) collective-permute-start(bf16[4,4096]{1,0:T(4,128)(2,1)S(1)} %get-tuple-element.50), channel_id=1, source_target_pairs={{0,26},{2,24},{4,30},{6,28},{8,18},{10,16},{12,22},{14,20},{16,10}... | collective-permute-start | bytes 98312 | tf_op jit(solution)/shard_map/ppermute | solution.py:32
  32.5 0.0 collective-permute-start.13
  32.5 2.8 %collective-permute-start.14 = (bf16[4,4096]{1,0:T(4,128)(2,1)S(1)}, bf16[4,4096]{1,0:T(4,128)(2,1)S(1)}, u32[]{:S(2)}, u32[]{:S(2)}) collective-permute-start(bf16[4,4096]{1,0:T(4,128)(2,1)S(1)} %get-tuple-element.52), channel_id=1, source_target_pairs={{0,10},{2,8},{4,14},{6,12},{8,2},{10,0},{12,6},{14,4},{16,26},{18,... | collective-permute-start | bytes 98312 | tf_op jit(solution)/shard_map/ppermute | solution.py:32
  35.2 0.3 collective-permute-start.8
  35.5 0.6 %shard_map.98 = (bf16[32,256]{1,0:T(8,128)(2,1)S(1)}, f32[40,256]{1,0:T(8,128)S(1)}, f32[1,256]{1,0:T(1,128)}, f32[1,256]{1,0:T(1,128)S(1)}) custom-call(f32[32,512]{1,0:T(8,128)S(1)} %get-tuple-element.33.raw_ref, f32[32,128]{1,0:T(8,128)S(1)} %get-tuple-element.34.scale_ref, f32[32,512]{1,0:T(8,128)S(1)} %get-tuple-element.38.coef_ref, ...), custom_call_target="tpu_custom_call" | custom-call | flops 200000 | bytes 1000000 | tf_op jit(solution)/shard_map/pallas_call | solution.py:41
  36.1 0.2 collective-permute-start.9
  36.3 0.1 collective-permute-done.12
  36.4 1.7 %collective-permute-done.13 = bf16[4,4096]{1,0:T(4,128)(2,1)S(1)} collective-permute-done((bf16[4,4096]{1,0:T(4,128)(2,1)S(1)}, bf16[4,4096]{1,0:T(4,128)(2,1)S(1)}, u32[]{:S(2)}, u32[]{:S(2)}) %collective-permute-start.13) | collective-permute-done | bytes 32800 | tf_op jit(solution)/shard_map/ppermute | solution.py:32
  38.1 0.0 collective-permute-done.14
  38.2 1.6 %collective-permute-start.15 = (bf16[4,4096]{1,0:T(4,128)(2,1)S(1)}, bf16[4,4096]{1,0:T(4,128)(2,1)S(1)}, u32[]{:S(2)}, u32[]{:S(2)}) collective-permute-start(bf16[4,4096]{1,0:T(4,128)(2,1)S(1)} %get-tuple-element.53), channel_id=1, source_target_pairs={{0,1},{1,0},{2,3},{3,2},{4,5},{5,4},{6,7},{7,6},{8,9},{9,8},{10,11... | collective-permute-start | bytes 98312 | tf_op jit(solution)/shard_map/ppermute | solution.py:32
  39.7 2.4 %collective-permute-done.15.refs_0_ = bf16[4,4096]{1,0:T(4,128)(2,1)S(1)} collective-permute-done((bf16[4,4096]{1,0:T(4,128)(2,1)S(1)}, bf16[4,4096]{1,0:T(4,128)(2,1)S(1)}, u32[]{:S(2)}, u32[]{:S(2)}) %collective-permute-start.15) | collective-permute-done | bytes 32800 | tf_op jit(solution)/shard_map/ppermute | solution.py:32
  42.1 0.9 %shard_map.103 = bf16[4,4096]{1,0:T(4,128)(2,1)} custom-call(bf16[4,4096]{1,0:T(4,128)(2,1)S(1)} %copy-done.1, f32[4,4096]{1,0:T(4,128)S(1)} %get-tuple-element.54.total_ref, bf16[4,4096]{1,0:T(4,128)(2,1)S(1)} %collective-permute-done.15.refs_0_), custom_call_target="tpu_custom_call" | custom-call | flops 200000 | bytes 1000000 | tf_op jit(solution)/shard_map/pallas_call | solution.py:41
  43.0 0.0 collective-permute-done.9.refs_3_
  43.0 0.0 collective-permute-done.8.refs_1_
  43.0 2.3 %shard_map.99.refs_7_ = bf16[256,4096]{1,0:T(8,128)(2,1)} custom-call(bf16[32,4096]{1,0:T(8,128)(2,1)S(1)} %get-tuple-element.41.refs_0_, bf16[32,4096]{1,0:T(8,128)(2,1)S(1)} %collective-permute-done.8.refs_1_, bf16[32,256]{1,0:T(8,128)(2,1)S(1)} %get-tuple-element.42.refs_2_, f32[40,256]{1,0:T(8,128)S(1)} %collective-permute-done.9.refs_3_, ...), custom_call_target="tpu_custom_call" | custom-call | flops 67108864 | bytes 3000000 | tf_op jit(solution)/shard_map/pallas_call | solution.py:41
  45.3 2.3 %shard_map.100 = bf16[256,4096]{1,0:T(8,128)(2,1)} custom-call(bf16[32,4096]{1,0:T(8,128)(2,1)S(1)} %get-tuple-element.41.refs_0_, bf16[32,4096]{1,0:T(8,128)(2,1)S(1)} %collective-permute-done.8.refs_1_, bf16[32,256]{1,0:T(8,128)(2,1)S(1)} %get-tuple-element.42.refs_2_, ...), custom_call_target="tpu_custom_call", output_to_operand_aliasing={{}: (7, {})} | custom-call | flops 67108864 | bytes 3000000 | tf_op jit(solution)/shard_map/pallas_call | solution.py:41
  (7 shorter events, 0.1 us)
Async XLA Ops:
  0.6 14.5 %copy-start = (bf16[256,4096]{1,0:T(8,128)(2,1)S(1)}, bf16[256,4096]{1,0:T(8,128)(2,1)}, u32[]{:S(2)}) copy-start(bf16[256,4096]{1,0:T(8,128)(2,1)} %q_ref.1) | copy-start | bytes 6291460
  0.6 14.5 %collective-permute-start.5 = (bf16[256,4096]{1,0:T(8,128)(2,1)}, bf16[256,4096]{1,0:T(8,128)(2,1)}, u32[]{:S(2)}, u32[]{:S(2)}) collective-permute-start(bf16[256,4096]{1,0:T(8,128)(2,1)} %q_ref.1), channel_id=1, source_target_pairs={{0,2},{2,0},{4,6},{6,4},{8,10},{10,8},{12,14},{14,12},{16,18},{18,... | collective-permute-start | bytes 6291464 | tf_op jit(solution)/shard_map/ppermute | solution.py:32
  1.2 5.6 %collective-permute-start.1 = (bf16[4,4096]{1,0:T(4,128)(2,1)}, bf16[4,4096]{1,0:T(4,128)(2,1)S(1)}, u32[]{:S(2)}, u32[]{:S(2)}) collective-permute-start(bf16[4,4096]{1,0:T(4,128)(2,1)} %p_ref.1), channel_id=1, source_target_pairs={{0,18},{2,16},{4,22},{6,20},{8,26},{10,24},{12,30},{14,28},{16,2},... | collective-permute-start | bytes 98312 | tf_op jit(solution)/shard_map/ppermute | solution.py:32
  4.9 5.5 %collective-permute-start.2 = (bf16[4,4096]{1,0:T(4,128)(2,1)}, bf16[4,4096]{1,0:T(4,128)(2,1)S(1)}, u32[]{:S(2)}, u32[]{:S(2)}) collective-permute-start(bf16[4,4096]{1,0:T(4,128)(2,1)} %p_ref.1), channel_id=1, source_target_pairs={{0,26},{2,24},{4,30},{6,28},{8,18},{10,16},{12,22},{14,20},{16,10}... | collective-permute-start | bytes 98312 | tf_op jit(solution)/shard_map/ppermute | solution.py:32
  5.9 6.0 %collective-permute-start = (bf16[4,4096]{1,0:T(4,128)(2,1)}, bf16[4,4096]{1,0:T(4,128)(2,1)S(1)}, u32[]{:S(2)}, u32[]{:S(2)}) collective-permute-start(bf16[4,4096]{1,0:T(4,128)(2,1)} %p_ref.1), channel_id=1, source_target_pairs={{0,10},{2,8},{4,14},{6,12},{8,2},{10,0},{12,6},{14,4},{16,26},{18,... | collective-permute-start | bytes 98312 | tf_op jit(solution)/shard_map/ppermute | solution.py:32
  10.5 7.5 %collective-permute-start.4 = (bf16[8,4096]{1,0:T(8,128)(2,1)S(1)}, bf16[8,4096]{1,0:T(8,128)(2,1)S(1)}, u32[]{:S(2)}, u32[]{:S(2)}) collective-permute-start(bf16[8,4096]{1,0:T(8,128)(2,1)S(1)} %pad_maximum_fusion.1.refs_1_), channel_id=1, source_target_pairs={{0,6},{2,4},{4,2},{6,0},{8,14},{10,12},{12,10},{14,8},{16,22},{18,... | collective-permute-start | bytes 196616 | tf_op jit(solution)/shard_map/ppermute | solution.py:32
  12.7 5.3 %collective-permute-start.3 = (bf16[8,4096]{1,0:T(8,128)(2,1)S(1)}, bf16[8,4096]{1,0:T(8,128)(2,1)S(1)}, u32[]{:S(2)}, u32[]{:S(2)}) collective-permute-start(bf16[8,4096]{1,0:T(8,128)(2,1)S(1)} %pad_maximum_fusion.refs_0_), channel_id=1, source_target_pairs={{0,6},{2,4},{4,2},{6,0},{8,14},{10,12},{12,10},{14,8},{16,22},{18,... | collective-permute-start | bytes 196616 | tf_op jit(solution)/shard_map/ppermute | solution.py:32
  14.8 3.2 %copy-start.2 = (f32[32,256]{1,0:T(8,128)S(1)}, f32[32,256]{1,0:T(8,128)}, u32[]{:S(2)}) copy-start(f32[32,256]{1,0:T(8,128)} %get-tuple-element.31.refs_9_) | copy-start | bytes 98308
  14.8 3.1 %copy-start.3 = (s32[256]{0:T(256)S(1)}, s32[256]{0:T(256)}, u32[]{:S(2)}) copy-start(s32[256]{0:T(256)} %param.9) | copy-start | bytes 3076
  14.8 3.1 %collective-permute-start.6 = (f32[40,256]{1,0:T(8,128)}, f32[40,256]{1,0:T(8,128)S(1)}, u32[]{:S(2)}, u32[]{:S(2)}) collective-permute-start(f32[40,256]{1,0:T(8,128)} %get-tuple-element.32), channel_id=1, source_target_pairs={{0,2},{2,0},{4,6},{6,4},{8,10},{10,8},{12,14},{14,12},{16,18},{18,... | collective-permute-start | bytes 122888 | tf_op jit(solution)/shard_map/ppermute | solution.py:32
  18.0 4.1 %copy-start.4 = (f32[256]{0:T(256)S(1)}, f32[256]{0:T(256)}, u32[]{:S(2)}) copy-start(f32[256]{0:T(256)} %param.13) | copy-start | bytes 3076
  20.8 1.2 %collective-permute-start.7 = (f32[8,512]{1,0:T(8,128)S(1)}, f32[8,512]{1,0:T(8,128)S(1)}, u32[]{:S(2)}, u32[]{:S(2)}) collective-permute-start(f32[8,512]{1,0:T(8,128)S(1)} %get-tuple-element.37.refs_5_), channel_id=1, source_target_pairs={{0,2},{2,0},{4,6},{6,4},{8,10},{10,8},{12,14},{14,12},{16,18},{18,... | collective-permute-start | bytes 49160 | tf_op jit(solution)/shard_map/ppermute | solution.py:32
  24.3 6.9 %collective-permute-start.10 = (bf16[16,2816]{1,0:T(8,128)(2,1)S(1)}, bf16[16,2816]{1,0:T(8,128)(2,1)S(1)}, u32[]{:S(2)}, u32[]{:S(2)}) collective-permute-start(bf16[16,2816]{1,0:T(8,128)(2,1)S(1)} %get-tuple-element.47), channel_id=1, source_target_pairs={{0,6},{2,4},{4,2},{6,0},{8,14},{10,12},{12,10},{14,8},{16,22},{18,... | collective-permute-start | bytes 270344 | tf_op jit(solution)/shard_map/ppermute | solution.py:32
  25.7 16.4 %copy-start.1 = (bf16[4,4096]{1,0:T(4,128)(2,1)S(1)}, bf16[4,4096]{1,0:T(4,128)(2,1)}, u32[]{:S(2)}) copy-start(bf16[4,4096]{1,0:T(4,128)(2,1)} %p_ref.1) | copy-start | bytes 98308
  27.7 3.5 %collective-permute-start.11 = (bf16[16,1280]{1,0:T(8,128)(2,1)S(1)}, bf16[16,1280]{1,0:T(8,128)(2,1)S(1)}, u32[]{:S(2)}, u32[]{:S(2)}) collective-permute-start(bf16[16,1280]{1,0:T(8,128)(2,1)S(1)} %get-tuple-element.48), channel_id=1, source_target_pairs={{0,6},{2,4},{4,2},{6,0},{8,14},{10,12},{12,10},{14,8},{16,22},{18,... | collective-permute-start | bytes 122888 | tf_op jit(solution)/shard_map/ppermute | solution.py:32
  31.2 5.2 %collective-permute-start.12 = (bf16[4,4096]{1,0:T(4,128)(2,1)S(1)}, bf16[4,4096]{1,0:T(4,128)(2,1)S(1)}, u32[]{:S(2)}, u32[]{:S(2)}) collective-permute-start(bf16[4,4096]{1,0:T(4,128)(2,1)S(1)} %get-tuple-element.50), channel_id=1, source_target_pairs={{0,26},{2,24},{4,30},{6,28},{8,18},{10,16},{12,22},{14,20},{16,10}... | collective-permute-start | bytes 98312 | tf_op jit(solution)/shard_map/ppermute | solution.py:32
  32.5 5.7 %collective-permute-start.13 = (bf16[4,4096]{1,0:T(4,128)(2,1)S(1)}, bf16[4,4096]{1,0:T(4,128)(2,1)S(1)}, u32[]{:S(2)}, u32[]{:S(2)}) collective-permute-start(bf16[4,4096]{1,0:T(4,128)(2,1)S(1)} %get-tuple-element.51), channel_id=1, source_target_pairs={{0,18},{2,16},{4,22},{6,20},{8,26},{10,24},{12,30},{14,28},{16,2},... | collective-permute-start | bytes 98312 | tf_op jit(solution)/shard_map/ppermute | solution.py:32
  32.5 5.7 %collective-permute-start.14 = (bf16[4,4096]{1,0:T(4,128)(2,1)S(1)}, bf16[4,4096]{1,0:T(4,128)(2,1)S(1)}, u32[]{:S(2)}, u32[]{:S(2)}) collective-permute-start(bf16[4,4096]{1,0:T(4,128)(2,1)S(1)} %get-tuple-element.52), channel_id=1, source_target_pairs={{0,10},{2,8},{4,14},{6,12},{8,2},{10,0},{12,6},{14,4},{16,26},{18,... | collective-permute-start | bytes 98312 | tf_op jit(solution)/shard_map/ppermute | solution.py:32
  35.2 7.8 %collective-permute-start.8 = (bf16[32,4096]{1,0:T(8,128)(2,1)S(1)}, bf16[32,4096]{1,0:T(8,128)(2,1)S(1)}, u32[]{:S(2)}, u32[]{:S(2)}) collective-permute-start(bf16[32,4096]{1,0:T(8,128)(2,1)S(1)} %get-tuple-element.41.refs_0_), channel_id=1, source_target_pairs={{0,2},{2,0},{4,6},{6,4},{8,10},{10,8},{12,14},{14,12},{16,18},{18,... | collective-permute-start | bytes 786440 | tf_op jit(solution)/shard_map/ppermute | solution.py:32
  36.1 7.0 %collective-permute-start.9 = (f32[40,256]{1,0:T(8,128)S(1)}, f32[40,256]{1,0:T(8,128)S(1)}, u32[]{:S(2)}, u32[]{:S(2)}) collective-permute-start(f32[40,256]{1,0:T(8,128)S(1)} %get-tuple-element.43), channel_id=1, source_target_pairs={{0,2},{2,0},{4,6},{6,4},{8,10},{10,8},{12,14},{14,12},{16,18},{18,... | collective-permute-start | bytes 122888 | tf_op jit(solution)/shard_map/ppermute | solution.py:32
  38.2 4.0 %collective-permute-start.15 = (bf16[4,4096]{1,0:T(4,128)(2,1)S(1)}, bf16[4,4096]{1,0:T(4,128)(2,1)S(1)}, u32[]{:S(2)}, u32[]{:S(2)}) collective-permute-start(bf16[4,4096]{1,0:T(4,128)(2,1)S(1)} %get-tuple-element.53), channel_id=1, source_target_pairs={{0,1},{1,0},{2,3},{3,2},{4,5},{5,4},{6,7},{7,6},{8,9},{9,8},{10,11... | collective-permute-start | bytes 98312 | tf_op jit(solution)/shard_map/ppermute | solution.py:32
